TPU v7x, 512 devices: a whole 4x4x16 slice. The times are simulated.
512 devices in a mesh: sample: 32 (over x, y, core), cls: 16 (over z).
Axes of the slice: x: 4, y: 4, z: 16, core: 2. Of those that a mesh axis runs over, the one named last changes fastest.
Arguments:
- features: bfloat16 [16384, 2048], P('sample', 'cls'), may hold values from -1.5 to 1.5
- head: bfloat16 [2048, 8192], P('sample', 'cls'), may hold values from -1.5859375 to 1.5859375
- class_cap: bfloat16 [8192], P('cls'), may hold values from 0.5 to 4
Outputs:
- targets: bfloat16 [16384, 8192], P('sample', 'cls')
- grad_features: bfloat16 [16384, 2048], P('sample', 'cls')
- grad_head: bfloat16 [2048, 8192], P('sample', 'cls')
All inputs are finite; a program needn't handle non-finite values.
Results may differ from a plain program's by a relative error of at most 0.02.
Values may be sent and summed in bfloat16 or wider, within the bound.
A program may use at most 64 MiB of HBM per device.

v0:
```python
import jax
import jax.numpy as jnp
from jax import lax
from jax.sharding import PartitionSpec as P

ITERS = 3


softcap = 15.0
sharpen = 2.0


def row_total(values):
    return lax.psum(jnp.sum(values, axis=1), "cls")


def per_device(features, head, class_cap):
    local_rows = features.shape[0]
    class_local = head.shape[1]
    sample_count = lax.axis_size("sample")
    class_groups = lax.axis_size("cls")
    ratio = local_rows * sample_count / (class_local * class_groups)
    whole = lax.all_gather(features, "cls", axis=1, tiled=True)
    head_full = lax.all_gather(head, "sample", axis=0, tiled=True)
    logits = jnp.dot(whole, head_full, preferred_element_type=jnp.float32)
    capped = softcap * jnp.tanh(logits / softcap)
    student = jnp.exp(capped)
    transport = jnp.exp(capped * sharpen)
    student_mass, plan_mass = lax.psum(
        (jnp.sum(student, axis=1), jnp.sum(transport, axis=1)), "cls"
    )
    student = student / student_mass[:, None]
    ceiling = class_cap.astype(jnp.float32) * ratio
    for iteration in range(ITERS):
        if iteration > 0:
            plan_mass = row_total(transport)
        transport = transport / plan_mass[:, None]
        column_mass = lax.psum(jnp.sum(transport, axis=0), "sample")
        transport = transport * jnp.minimum(1.0, ceiling / column_mass)
    targets = (transport / row_total(transport)[:, None]).astype(jnp.bfloat16)
    tanh_slope = 1.0 - (capped / softcap) ** 2
    grad_logits = ((student - targets.astype(jnp.float32)) * tanh_slope).astype(jnp.bfloat16)
    grad_head = lax.psum_scatter(
        lax.dot_general(
            whole, grad_logits, (((0,), (0,)), ((), ())), preferred_element_type=jnp.float32
        ).astype(jnp.bfloat16),
        "sample",
        scatter_dimension=0,
        tiled=True,
    )
    share = lax.psum_scatter(
        lax.dot_general(
            head_full, grad_logits, (((1,), (1,)), ((), ())), preferred_element_type=jnp.float32
        ).astype(jnp.bfloat16),
        "cls",
        scatter_dimension=0,
        tiled=True,
    ).astype(jnp.float32)
    grad_features = jnp.transpose(share).astype(jnp.bfloat16)
    return (targets, grad_features, grad_head)


def solution(mesh):
    return jax.shard_map(
        per_device,
        mesh=mesh,
        in_specs=(P("sample", "cls"), P("sample", "cls"), P("cls")),
        out_specs=(P("sample", "cls"), P("sample", "cls"), P("sample", "cls")),
        check_vma=False,
    )
```

profile of v0, /device:TPU:4, one launch (start us, length us, event | category | flops | bytes accessed | tf_op | source)
XLA Modules:
  0.0 643.5 jit_solution(15477664846677126857)
XLA Ops:
  7.2 0.0 all-gather.3.cloned.1.call-start
  7.2 0.7 all-gather.3.cloned.1.call-update
  7.9 0.0 all-gather.5.cloned.1.call-start
  7.9 0.7 all-gather.5.cloned.1.call-update
  8.6 0.0 copy-start
  8.7 0.0 reduce-scatter.7.cloned.1.call-start
  8.7 85.0 %all-gather.3.cloned.1.call-done = bf16[512,2048]{1,0:T(8,128)(2,1)} async-done(((bf16[512,128]{1,0:T(8,128)(2,1)}), bf16[512,2048]{1,0:T(8,128)(2,1)}) %all-gather.3.cloned.1.call-update) | async-done | bytes 2097168 | tf_op jit(solution)/shard_map/all_gather | solution.py:23
  93.7 57.0 %all-gather.5.cloned.1.call-done = bf16[2048,512]{1,0:T(8,128)(2,1)} async-done(((bf16[64,512]{1,0:T(8,128)(2,1)}), bf16[2048,512]{1,0:T(8,128)(2,1)}) %all-gather.5.cloned.1.call-update) | async-done | bytes 2097168 | tf_op jit(solution)/shard_map/all_gather | solution.py:24
  150.7 3.7 fusion.5
  154.3 31.3 %psum.56 = f32[512]{0:T(512)S(1)} all-reduce(f32[512]{0:T(512)S(1)} %get-tuple-element.17), channel_id=1, replica_groups=mesh['sample'=32,'cls'=16] {'cls'}, use_global_device_ids=true, to_apply=%region_1.0 | all-reduce | flops 512 | bytes 4096 | tf_op jit(solution)/shard_map/psum | solution.py:29
  185.6 0.3 fusion.12
  185.9 53.0 %psum.57 = f32[512]{0:T(512)S(1)} all-reduce(f32[512]{0:T(512)S(1)} %fusion.12), channel_id=1, replica_groups=mesh['sample'=32,'cls'=16] {'sample'}, use_global_device_ids=true, to_apply=%region_3.0 | all-reduce | flops 512 | bytes 4096 | tf_op jit(solution)/shard_map/psum | solution.py:38
  238.9 0.0 copy-done
  238.9 0.4 fusion.3
  239.2 28.4 %psum.58 = f32[512]{0:T(512)S(1)} all-reduce(f32[512]{0:T(512)S(1)} %get-tuple-element.10), channel_id=1, replica_groups=mesh['sample'=32,'cls'=16] {'cls'}, use_global_device_ids=true, to_apply=%region_5.0 | all-reduce | flops 512 | bytes 4096 | tf_op jit(solution)/shard_map/psum | solution.py:14
  267.6 0.3 fusion.14
  268.0 53.0 %psum.59 = f32[512]{0:T(512)S(1)} all-reduce(f32[512]{0:T(512)S(1)} %get-tuple-element.15), channel_id=1, replica_groups=mesh['sample'=32,'cls'=16] {'sample'}, use_global_device_ids=true, to_apply=%region_7.0 | all-reduce | flops 512 | bytes 4096 | tf_op jit(solution)/shard_map/psum | solution.py:38
  321.0 0.2 multiply_reduce_fusion.1
  321.1 28.9 %psum.60 = f32[512]{0:T(512)S(1)} all-reduce(f32[512]{0:T(512)S(1)} %multiply_reduce_fusion.1), channel_id=1, replica_groups=mesh['sample'=32,'cls'=16] {'cls'}, use_global_device_ids=true, to_apply=%region_9.0 | all-reduce | flops 512 | bytes 4096 | tf_op jit(solution)/shard_map/psum | solution.py:14
  350.0 0.3 fusion.13
  350.3 53.0 %psum.61 = f32[512]{0:T(512)S(1)} all-reduce(f32[512]{0:T(512)S(1)} %fusion.13), channel_id=1, replica_groups=mesh['sample'=32,'cls'=16] {'sample'}, use_global_device_ids=true, to_apply=%region_11.0 | all-reduce | flops 512 | bytes 4096 | tf_op jit(solution)/shard_map/psum | solution.py:38
  403.3 0.2 multiply_reduce_fusion
  403.5 27.9 %all-reduce = (f32[512]{0:T(512)S(1)}, f32[512]{0:T(512)S(1)}) all-reduce(f32[512]{0:T(512)S(1)} %multiply_reduce_fusion, f32[512]{0:T(512)S(1)} %get-tuple-element.9), channel_id=1, replica_groups=mesh['sample'=32,'cls'=16] {'cls'}, use_global_device_ids=true, to_apply=%region_13.0 | all-reduce | flops 1024 | bytes 8192 | tf_op jit(solution)/shard_map/psum | solution.py:14
  431.4 0.0 copy-start.1
  431.4 0.5 multiply_convert_fusion
  431.9 1.1 copy-done.1
  433.0 1.3 fusion
  434.3 2.6 copy.10
  436.9 0.0 reduce-scatter.7.cloned.1.call-update
  436.9 0.0 reduce-scatter.9.cloned.1.call-start
  436.9 2.8 fusion.1
  439.8 2.5 copy.12
  442.3 0.0 reduce-scatter.9.cloned.1.call-update
  442.3 1.0 copy.8
  443.3 89.5 %reduce-scatter.7.cloned.1.call-done = bf16[128,512]{1,0:T(8,128)(2,1)} async-done(((bf16[2048,512]{1,0:T(8,128)(2,1)}), bf16[128,512]{1,0:T(8,128)(2,1)}) %reduce-scatter.7.cloned.1.call-update) | async-done | bytes 131088
  532.9 1.7 copy.11
  534.5 102.4 %reduce-scatter.9.cloned.1.call-done = bf16[64,512]{1,0:T(8,128)(2,1)} async-done(((bf16[2048,512]{1,0:T(8,128)(2,1)}), bf16[64,512]{1,0:T(8,128)(2,1)}) %reduce-scatter.9.cloned.1.call-update) | async-done | bytes 65552
  (3 shorter events, 0.0 us)
Async XLA Ops:
  7.2 86.6 %all-gather.3.cloned.1.call-start = ((), (), s32[]{:S(2)}) async-start(), calls=%async_computation.2 | async-start | bytes 2228224 | tf_op jit(solution)/shard_map/all_gather | solution.py:23
  7.9 142.8 %all-gather.5.cloned.1.call-start = ((), (), s32[]{:S(2)}) async-start(), calls=%async_computation.3 | async-start | bytes 2162688 | tf_op jit(solution)/shard_map/all_gather | solution.py:24
  8.6 230.2 %copy-start = (bf16[512]{0:T(512)(128)(2,1)S(1)}, bf16[512]{0:T(512)(128)(2,1)}, u32[]{:S(2)}) copy-start(bf16[512]{0:T(512)(128)(2,1)} %param.5) | copy-start | bytes 3076
  8.7 524.2 %reduce-scatter.7.cloned.1.call-start = ((), (), s32[]{:S(2)}) async-start(), calls=%async_computation.4 | async-start | bytes 2228224
  431.4 1.6 copy-start.1
  436.9 200.0 %reduce-scatter.9.cloned.1.call-start = ((), (), s32[]{:S(2)}) async-start(), calls=%async_computation.5 | async-start | bytes 2162688
Sparse Core Ops, SparseCore 0:
  10.0 83.6 all-gather.2
  96.8 53.7 all-gather.4
  437.0 95.8 reduce-scatter.6
  537.7 99.1 reduce-scatter.8
where the time goes:
time: 644 us; the launch traced here: 643 us
  waiting for transfers between devices  335 us (52%)
  blocking collectives  275 us (43%)
  between operations  13.8 us (2%)
  local copies, waits for them, and re-layouts  8.86 us (1%)
  matrix products  7.85 us (1%)
    unnamed x6, waiting for transfers between devices  193 us
    psum x3, blocking collectives, per_device(): column_mass = lax.psum(jnp.sum(transport, axis=0), 'sample')  159 us
    psum x3, blocking collectives, row_total(): return lax.psum(jnp.sum(values, axis=1), 'cls')  85.2 us
    all_gather x1, waiting for transfers between devices, per_device(): whole = lax.all_gather(features, 'cls', axis=1, tiled=True)  85 us
    all_gather x1, waiting for transfers between devices, per_device(): head_full = lax.all_gather(head, 'sample', axis=0, tiled=True)  57 us
    psum x1, blocking collectives, per_device(): lax.psum((jnp.sum(student, axis=1), jnp.sum(transport, axis=1)), 'cls')  31.3 us
  transfers between devices with their start and end apart: 4, of which 4 were waited for; matrix products, arithmetic and copies ran while one was open for 1% of the time, Pallas kernels for 0%

commit v1 on v0

v1 whole, which is shorter than its diff:
```python
import functools
import jax
import jax.numpy as jnp
from jax import lax
from jax.experimental import pallas as pl
from jax.experimental.pallas import tpu as pltpu
from jax.sharding import PartitionSpec as P

ITERS = 3
softcap = 15.0
sharpen = 2.0
MESH = pl.DeviceIdType.MESH
SIDE = 4
BF = jnp.bfloat16
F32 = jnp.float32

OTHERS = sorted(
    ((dx, dy, dc) for dx in range(SIDE) for dy in range(SIDE) for dc in range(2) if dx or dy or dc),
    key=lambda o: -(min(o[0], SIDE - o[0]) + min(o[1], SIDE - o[1]) + 0.5 * o[2]),
)


def kernel(
    rows, width, classes, groups, ratio,
    feat, head, cap,
    tgt, gfeat, ghead,
    fs, hs, ft, ht, acc, stu, plan, slope, grad, rrep,
    part, from_l, from_r,
    qo, core_in, qa, y_in, qb, x_in,
    zs0, zs, zr0, zr, cs, cr,
    ag_send, ag_recv, hx_send, hx_recv, hy_send, hy_recv, hc_send, hc_recv,
    zsend, zrecv, csend, crecv,
    rs_send, rs_recv, qc_send, qc_recv, qy_send, qy_recv, qx_send, qx_recv,
):
    s = lax.axis_index("sample")
    z = lax.axis_index("cls")
    core = lax.rem(s, 2)
    chip = s // 2
    y = lax.rem(chip, SIDE)
    x = chip // SIDE
    way = 1 - 2 * core
    half = rows // 2
    slab = width // groups
    far = groups // 2

    def at(dx, dy, flip=0):
        c = lax.rem(core + flip, 2)
        return ((lax.rem(x + dx + SIDE, SIDE) * SIDE + lax.rem(y + dy + SIDE, SIDE)) * 2 + c, z)

    def along(d):
        return (s, lax.rem(z + d + groups, groups))

    def slot(dx, dy):
        return (lax.rem(x + dx + SIDE, SIDE) * SIDE + lax.rem(y + dy + SIDE, SIDE)) * 2 + core

    def copy(src, dst, ssem, rsem, to):
        return pltpu.make_async_remote_copy(
            src_ref=src, dst_ref=dst, send_sem=ssem, recv_sem=rsem, device_id=to, device_id_type=MESH
        )

    sent = []

    def send(src, dst, ssem, rsem, to):
        c = copy(src, dst, ssem, rsem, to)
        c.start()
        sent.append(c)

    def arrived(ref, rsem):
        copy(ref, ref, rsem, rsem, along(1)).wait_recv()

    barrier = pltpu.get_barrier_semaphore()
    near = [along(1), along(-1), at(1, 0), at(-1, 0), at(0, 1), at(0, -1), at(0, 0, 1)]
    for to in near:
        pl.semaphore_signal(barrier, inc=1, device_id=to, device_id_type=MESH)
    pl.semaphore_wait(barrier, len(near))

    def part_of(ref, h):
        return ref.at[pl.ds(h * half, half)]

    def ring_send(t, h, forward):
        hop = 1 if forward else -1
        k = lax.rem(z - hop * t + groups, groups)
        src = part_of(feat, h) if t == 0 else part_of(fs.at[k], h)
        i = 0 if forward else 1
        send(src, part_of(fs.at[k], h), ag_send.at[i, t, h], ag_recv.at[i, t, h], along(hop))

    def ring_wait(t, h, forward):
        hop = 1 if forward else -1
        k = lax.rem(z - hop * (t + 1) + groups, groups)
        arrived(part_of(fs.at[k], h), ag_recv.at[0 if forward else 1, t, h])

    def ring_step(t):
        for h in range(2):
            for forward in (True, False):
                ring_wait(t - 1, h, forward)
                if t < far - 1 or (h == 0) == forward:
                    ring_send(t, h, forward)

    x_off = (0, -1, 1, 2)
    own = 2 * chip + core

    def to_y(j, src):
        k = slot(x_off[j], 0)
        send(src, hs.at[k], hy_send.at[j, 0], hy_recv.at[j, 0], at(0, 1))
        send(src, hs.at[k], hy_send.at[j, 1], hy_recv.at[j, 1], at(0, -1))

    def to_core(j, i, src):
        k = slot(x_off[j], x_off[i])
        send(src, hs.at[k], hc_send.at[j, i], hc_recv.at[j, i], at(0, 0, 1))

    for h in range(2):
        ring_send(0, h, True)
        ring_send(0, h, False)
    send(head, hs.at[own], hx_send.at[0], hx_recv.at[0], at(1, 0))
    send(head, hs.at[own], hx_send.at[1], hx_recv.at[1], at(-1, 0))
    to_y(0, head)
    to_core(0, 0, head)
    fs[z] = feat[...]
    hs[own] = head[...]

    behind = slot(-way, 0)
    arrived(hs.at[behind], hx_recv.at[core])
    send(hs.at[behind], hs.at[behind], hx_send.at[2], hx_recv.at[2], at(way, 0))
    ahead = slot(way, 0)
    arrived(hs.at[ahead], hx_recv.at[1 - core])
    for j in (1, 2):
        to_y(j, hs.at[slot(x_off[j], 0)])
        to_core(j, 0, hs.at[slot(x_off[j], 0)])
    ring_step(1)
    arrived(hs.at[slot(2, 0)], hx_recv.at[2])
    to_y(3, hs.at[slot(2, 0)])
    to_core(3, 0, hs.at[slot(2, 0)])

    def y_pair(j):
        k = slot(x_off[j], -way)
        arrived(hs.at[k], hy_recv.at[j, core])
        send(hs.at[k], hs.at[k], hy_send.at[j, 2], hy_recv.at[j, 2], at(0, way))
        arrived(hs.at[slot(x_off[j], way)], hy_recv.at[j, 1 - core])
        to_core(j, 1, hs.at[slot(x_off[j], -1)])
        to_core(j, 2, hs.at[slot(x_off[j], 1)])

    def y_far(j):
        k = slot(x_off[j], 2)
        arrived(hs.at[k], hy_recv.at[j, 2])
        to_core(j, 3, hs.at[k])

    y_pair(0)
    ring_step(2)
    y_far(0)
    y_pair(1)
    ring_step(3)
    y_far(1)
    y_pair(2)
    ring_step(4)
    y_far(2)
    y_pair(3)
    ring_step(5)
    y_far(3)

    def head_of(k):
        return hs[pl.ds(2 * k, 2)].reshape(slab, classes)

    def logits_of(a, b, r0, n):
        left = jnp.concatenate([fs[a, pl.ds(r0, n), :], fs[b, pl.ds(r0, n), :]], axis=1)
        right = jnp.concatenate([head_of(a), head_of(b)], axis=0)
        return jnp.dot(left, right, preferred_element_type=F32)

    def around(d):
        return lax.rem(z - d + groups, groups), lax.rem(z + d, groups)

    ring_step(6)
    for j in range(4):
        for i in range(4):
            k = (lax.rem(x + x_off[j] + SIDE, SIDE) * SIDE + lax.rem(y + x_off[i] + SIDE, SIDE)) * 2 + (1 - core)
            arrived(hs.at[k], hc_recv.at[j, i])
    acc[...] = logits_of(*around(1), 0, rows)
    for d in (2, 3, 4):
        acc[...] += logits_of(*around(d), 0, rows)
    ring_step(7)
    for d in (5, 6, 7):
        acc[...] += logits_of(*around(d), 0, rows)
    ring_wait(far - 1, 0, True)
    ring_wait(far - 1, 1, False)

    lanes = 128
    tiles = classes // lanes

    def lane_tiles(v):
        return [v[:, i * lanes:(i + 1) * lanes] for i in range(tiles)]

    def turned_sum(v):
        return jnp.sum(sum(lane_tiles(v)[1:], lane_tiles(v)[0]).T, axis=0, keepdims=True)

    opposite = lax.rem(z + far, groups)
    for r0 in range(0, rows, lanes):
        block = pl.ds(r0, lanes)
        tanh = jnp.tanh((acc[block, :] + logits_of(z, opposite, r0, lanes)) / softcap)
        student = jnp.exp(softcap * tanh)
        transport = student * student
        stu[block, :] = student
        plan[block, :] = transport
        slope[block, :] = 1.0 - tanh * tanh
        zs0[:, r0:r0 + lanes] = turned_sum(transport)
        zs0[:, rows + r0:rows + r0 + lanes] = turned_sum(student)

    z_order = sorted(range(1, groups), key=lambda d: -min(d, groups - d))

    def z_exchange(mine, theirs, i):
        for d in z_order:
            copy(mine, theirs.at[d - 1], zsend.at[i], zrecv.at[i], along(d)).start()

    def z_total(mine, theirs, i):
        copy(theirs, theirs, zsend.at[i], zrecv.at[i], along(1)).wait_recv()
        return mine[...] + jnp.sum(theirs[...], axis=0)

    def c_exchange(mine, theirs, i):
        for n, (dx, dy, dc) in enumerate(OTHERS):
            copy(mine, theirs.at[n], csend.at[i], crecv.at[i], at(dx, dy, dc)).start()

    def c_total(mine, theirs, i):
        copy(theirs, theirs, csend.at[i], crecv.at[i], along(1)).wait_recv()
        return mine[...] + jnp.sum(theirs[...], axis=0)

    def upright(row, r0):
        return jnp.broadcast_to(row[:, r0:r0 + lanes], (lanes, lanes)).T

    z_exchange(zs0, zr0, 0)

    def turn(k, carry):
        t = fs[k].T
        ft[0, lax.rem(k, SIDE), k // SIDE] = t[: slab // 2]
        ft[1, lax.rem(k, SIDE), k // SIDE] = t[slab // 2:]
        ht[k] = head_of(k).T
        return carry

    lax.fori_loop(0, groups, turn, 0)

    ceiling = cap[...].astype(F32) * ratio
    scale = jnp.ones((1, classes), F32)
    both = z_total(zs0, zr0, 0)
    mass = both[:, :rows]
    student_mass = both[:, rows:]
    for it in range(ITERS):
        inverse = 1.0 / mass
        column = jnp.zeros((1, classes), F32)
        for r0 in range(0, rows, lanes):
            up = upright(inverse, r0)
            rep = jnp.concatenate([up] * tiles, axis=1)
            column += jnp.sum(plan[pl.ds(r0, lanes), :] * rep, axis=0, keepdims=True)
        cs[it] = column
        c_exchange(cs.at[it], cr.at[it], it)
        total = c_total(cs.at[it], cr.at[it], it)
        scale = jnp.minimum(scale, ceiling / total)
        for r0 in range(0, rows, lanes):
            zs[it, :, r0:r0 + lanes] = turned_sum(plan[pl.ds(r0, lanes), :] * scale)
        z_exchange(zs.at[it], zr.at[it], it + 1)
        mass = z_total(zs.at[it], zr.at[it], it + 1)

    inverse = 1.0 / mass
    student_inverse = 1.0 / student_mass
    for r0 in range(0, rows, lanes):
        block = pl.ds(r0, lanes)
        up = jnp.concatenate([upright(inverse, r0)] * tiles, axis=1)
        sup = jnp.concatenate([upright(student_inverse, r0)] * tiles, axis=1)
        targets = (plan[block, :] * up * scale).astype(BF)
        tgt[block, :] = targets
        grad[block, :] = ((stu[block, :] * sup - targets.astype(F32)) * slope[block, :]).astype(BF)

    def share_pair(d):
        right = lax.rem(z + d, groups)
        left = lax.rem(z - d + groups, groups) if d < far else z
        both = jnp.concatenate([ht[right], ht[left]], axis=1)
        out = jnp.dot(grad[...], both, preferred_element_type=F32).astype(BF)
        part[d] = out[:, :slab]
        part[groups - d if d < far else 0] = out[:, slab:]

    def rs_send_to(d, h, right):
        i = 0 if right else 1
        src = part.at[d if right or d == far else groups - d]
        dst = from_l if right else from_r
        send(part_of(src, h), part_of(dst.at[d - 1], h), rs_send.at[i, d - 1, h], rs_recv.at[i, d - 1, h],
             along(1 if right else -1))

    def rs_add(d, h, right):
        i = 0 if right else 1
        got = (from_l if right else from_r).at[d]
        mine = part.at[d if right else groups - d]
        arrived(part_of(got, h), rs_recv.at[i, d, h])
        at_h = pl.ds(h * half, half)
        mine[at_h, :] = (mine[at_h, :].astype(F32) + got[at_h, :].astype(F32)).astype(BF)
        rs_send_to(d, h, right)

    def rs_step(d):
        for h in range(2):
            for right in (True, False):
                if d < far - 1 or (h == 0) == right:
                    rs_add(d, h, right)

    def head_share(c, i):
        lhs = ft[c, lax.rem(y + i, SIDE)].reshape(SIDE * slab // 2, rows)
        out = jnp.dot(lhs, grad[...], preferred_element_type=F32).astype(BF)
        return out.reshape(SIDE, slab // 2, classes)

    share_pair(far)
    rs_send_to(far, 0, True)
    rs_send_to(far, 1, False)
    share_pair(far - 1)
    rs_send_to(far - 1, 1, True)
    rs_send_to(far - 1, 0, False)
    for i in (2, 1, 3, 0):
        qo[i] = head_share(1 - core, i)
        send(qo.at[i], core_in.at[i], qc_send.at[i], qc_recv.at[i], at(0, 0, 1))
    share_pair(6)
    rs_step(7)
    for i in (2, 1, 3, 0):
        qa[i] = head_share(core, i)
    share_pair(5)
    rs_step(6)

    def summed(*refs):
        out = refs[0].astype(F32)
        for r in refs[1:]:
            out = out + r.astype(F32)
        return out.astype(BF)

    fwd = 1 + 2 * core
    bwd = 3 - 2 * core
    for i in (2, 1, 3, 0):
        arrived(core_in.at[i], qc_recv.at[i])
        qa[i] = summed(qa[i], core_in[i])
        if i == 2:
            send(qa.at[2], y_in.at[0], qy_send.at[0], qy_recv.at[0], at(0, way))
        if i == 3:
            send(qa.at[bwd], y_in.at[1], qy_send.at[1], qy_recv.at[1], at(0, -way))
    share_pair(4)
    share_pair(3)
    rs_step(5)
    share_pair(2)
    share_pair(1)
    arrived(y_in.at[0], qy_recv.at[0])
    qa[fwd] = summed(qa[fwd], y_in[0])
    send(qa.at[fwd], y_in.at[2], qy_send.at[2], qy_recv.at[2], at(0, way))
    rs_step(4)
    rs_step(3)
    arrived(y_in.at[1], qy_recv.at[1])
    arrived(y_in.at[2], qy_recv.at[2])
    qb[...] = summed(qa[0], y_in[1], y_in[2])

    def x_of(d):
        return lax.rem(x + d + SIDE, SIDE)

    send(qb.at[x_of(2)], x_in.at[0], qx_send.at[0], qx_recv.at[0], at(way, 0))
    send(qb.at[x_of(-way)], x_in.at[1], qx_send.at[1], qx_recv.at[1], at(-way, 0))
    rs_step(2)
    arrived(x_in.at[0], qx_recv.at[0])
    qb[x_of(way)] = summed(qb[x_of(way)], x_in[0])
    send(qb.at[x_of(way)], x_in.at[2], qx_send.at[2], qx_recv.at[2], at(way, 0))
    rs_step(1)
    arrived(x_in.at[1], qx_recv.at[1])
    arrived(x_in.at[2], qx_recv.at[2])
    ghead[...] = summed(qb[x], x_in[1], x_in[2])
    for h in range(2):
        arrived(part_of(from_l.at[0], h), rs_recv.at[0, 0, h])
        arrived(part_of(from_r.at[0], h), rs_recv.at[1, 0, h])
    gfeat[...] = summed(part[0], from_l[0], from_r[0])

    copy(zr0, zr0, zsend.at[0], zrecv.at[0], along(1)).wait_send()
    for it in range(ITERS):
        copy(zr.at[it], zr.at[it], zsend.at[it + 1], zrecv.at[it + 1], along(1)).wait_send()
        copy(cr.at[it], cr.at[it], csend.at[it], crecv.at[it], along(1)).wait_send()
    for c in sent:
        c.wait_send()


def solution(mesh):
    groups = mesh.shape["cls"]
    samples = mesh.shape["sample"]

    def per_device(features, head, class_cap):
        rows, slab = features.shape
        depth, classes = head.shape
        width = slab * groups
        chips = samples // 2
        far = groups // 2
        ratio = rows * samples / (classes * groups)
        V = pltpu.VMEM
        dma = pltpu.SemaphoreType.DMA
        scratch = [
            V((groups, rows, slab), BF), V((samples, depth, classes), BF),
            V((2, SIDE, SIDE, depth, rows), BF), V((groups, classes, slab), BF),
            V((rows, classes), F32), V((rows, classes), F32), V((rows, classes), F32), V((rows, classes), F32),
            V((rows, classes), BF), V((8, 128), F32),
            V((groups, rows, slab), BF), V((far, rows, slab), BF), V((far, rows, slab), BF),
            V((SIDE, SIDE, depth, classes), BF), V((SIDE, SIDE, depth, classes), BF),
            V((SIDE, SIDE, depth, classes), BF), V((3, SIDE, depth, classes), BF),
            V((SIDE, depth, classes), BF), V((3, depth, classes), BF),
            V((1, 2 * rows), F32), V((ITERS, 1, rows), F32),
            V((groups - 1, 1, 2 * rows), F32), V((ITERS, groups - 1, 1, rows), F32),
            V((ITERS, 1, classes), F32), V((ITERS, samples - 1, 1, classes), F32),
            dma((2, far, 2)), dma((2, far, 2)), dma((3,)), dma((3,)), dma((4, 3)), dma((4, 3)), dma((4, 4)), dma((4, 4)),
            dma((ITERS + 1,)), dma((ITERS + 1,)), dma((ITERS,)), dma((ITERS,)),
            dma((2, far, 2)), dma((2, far, 2)), dma((4,)), dma((4,)), dma((3,)), dma((3,)), dma((3,)), dma((3,)),
        ]
        vmem = pl.BlockSpec(memory_space=pltpu.VMEM)
        return pl.pallas_call(
            functools.partial(kernel, rows, width, classes, groups, ratio),
            out_shape=(
                jax.ShapeDtypeStruct((rows, classes), BF),
                jax.ShapeDtypeStruct((rows, slab), BF),
                jax.ShapeDtypeStruct((depth, classes), BF),
            ),
            in_specs=[vmem] * 3,
            out_specs=(vmem,) * 3,
            scratch_shapes=scratch,
            compiler_params=pltpu.CompilerParams(
                collective_id=0, has_side_effects=True, vmem_limit_bytes=48 << 20
            ),
        )(features, head, class_cap.reshape(1, classes))

    return jax.shard_map(
        per_device,
        mesh=mesh,
        in_specs=(P("sample", "cls"), P("sample", "cls"), P("cls")),
        out_specs=(P("sample", "cls"), P("sample", "cls"), P("sample", "cls")),
        check_vma=False,
    )
```

time: 644 us -> 127 us (0.20)
  the two profiles are of different devices: /device:TPU:4 before, /device:TPU:8 now
where the time goes in v1:
time: 127 us
  Pallas kernels  122 us (96%)
  local copies, waits for them, and re-layouts  4.51 us (4%)
    pallas_call x1, Pallas kernels, per_device(): pl.pallas_call(functools.partial(kernel, rows, width, classes, groups, ra...  122 us
    unnamed x7, local copies, waits for them, and re-layouts  3.82 us

profile of v1, /device:TPU:8, one launch (start us, length us, event | category | flops | bytes accessed | tf_op | source)
XLA Modules:
  0.0 127.3 jit_solution(5339639395678404269)
XLA Ops:
  0.6 0.7 reshape.9.cap
  1.3 0.0 copy-start
  1.3 0.9 copy-done
  2.2 0.0 copy-start.1
  2.2 0.8 copy-done.1
  3.1 122.1 %shard_map.58 = (bf16[512,512]{1,0:T(8,128)(2,1)S(1)}, bf16[512,128]{1,0:T(8,128)(2,1)S(1)}, bf16[64,512]{1,0:T(8,128)(2,1)S(1)}) custom-call(bf16[512,128]{1,0:T(8,128)(2,1)S(1)} %copy-done, bf16[64,512]{1,0:T(8,128)(2,1)S(1)} %copy-done.1, bf16[1,512]{1,0:T(2,128)(2,1)S(1)} %reshape.9.cap), custom_call_target="tpu_custom_call" | custom-call | tf_op jit(solution)/shard_map/pallas_call | solution.py:405
  125.2 0.8 copy.9
  126.0 0.7 copy.10
  126.7 0.6 copy.11
Async XLA Ops:
  1.3 0.9 copy-start
  2.2 0.8 copy-start.1

commit v2 on v1

--- a/solution.py
+++ b/solution.py
@@ -11,6 +11,7 @@
 sharpen = 2.0
 MESH = pl.DeviceIdType.MESH
 SIDE = 4
+PIECES = 4
 BF = jnp.bfloat16
 F32 = jnp.float32
 
@@ -22,14 +23,14 @@
 
 def kernel(
     rows, width, classes, groups, ratio,
-    feat, head, cap,
+    feat, head, cap_in,
     tgt, gfeat, ghead,
-    fs, hs, ft, ht, acc, stu, plan, slope, grad, rrep,
+    fs, hs, ft, ht, acc, stu, plan, slope, grad,
     part, from_l, from_r,
     qo, core_in, qa, y_in, qb, x_in,
     zs0, zs, zr0, zr, cs, cr,
     ag_send, ag_recv, hx_send, hx_recv, hy_send, hy_recv, hc_send, hc_recv,
-    zsend, zrecv, csend, crecv,
+    zsend, zrecv, csend, crecv, cap, local,
     rs_send, rs_recv, qc_send, qc_recv, qy_send, qy_recv, qx_send, qx_recv,
 ):
     s = lax.axis_index("sample")
@@ -39,7 +40,7 @@
     y = lax.rem(chip, SIDE)
     x = chip // SIDE
     way = 1 - 2 * core
-    half = rows // 2
+    n = rows // PIECES
     slab = width // groups
     far = groups // 2
 
@@ -74,27 +75,33 @@
         pl.semaphore_signal(barrier, inc=1, device_id=to, device_id_type=MESH)
     pl.semaphore_wait(barrier, len(near))
 
-    def part_of(ref, h):
-        return ref.at[pl.ds(h * half, half)]
-
-    def ring_send(t, h, forward):
+    def part_of(ref, q):
+        return ref.at[pl.ds(q * n, n)]
+
+    right_order = tuple(range(PIECES))
+    left_order = right_order[PIECES // 2:] + right_order[:PIECES // 2]
+
+    def halfway(q, forward):
+        return (q < PIECES // 2) == forward
+
+    def ring_send(t, q, forward):
         hop = 1 if forward else -1
         k = lax.rem(z - hop * t + groups, groups)
-        src = part_of(feat, h) if t == 0 else part_of(fs.at[k], h)
+        src = part_of(feat, q) if t == 0 else part_of(fs.at[k], q)
         i = 0 if forward else 1
-        send(src, part_of(fs.at[k], h), ag_send.at[i, t, h], ag_recv.at[i, t, h], along(hop))
-
-    def ring_wait(t, h, forward):
+        send(src, part_of(fs.at[k], q), ag_send.at[i, t, q], ag_recv.at[i, t, q], along(hop))
+
+    def ring_wait(t, q, forward):
         hop = 1 if forward else -1
         k = lax.rem(z - hop * (t + 1) + groups, groups)
-        arrived(part_of(fs.at[k], h), ag_recv.at[0 if forward else 1, t, h])
-
-    def ring_step(t):
-        for h in range(2):
-            for forward in (True, False):
-                ring_wait(t - 1, h, forward)
-                if t < far - 1 or (h == 0) == forward:
-                    ring_send(t, h, forward)
+        arrived(part_of(fs.at[k], q), ag_recv.at[0 if forward else 1, t, q])
+
+    def ring_step(t, pieces=range(PIECES)):
+        for p in pieces:
+            for forward, q in ((True, right_order[p]), (False, left_order[p])):
+                ring_wait(t - 1, q, forward)
+                if t < far - 1 or halfway(q, forward):
+                    ring_send(t, q, forward)
 
     x_off = (0, -1, 1, 2)
     own = 2 * chip + core
@@ -108,28 +115,34 @@
         k = slot(x_off[j], x_off[i])
         send(src, hs.at[k], hc_send.at[j, i], hc_recv.at[j, i], at(0, 0, 1))
 
-    for h in range(2):
-        ring_send(0, h, True)
-        ring_send(0, h, False)
+    for p in range(PIECES):
+        ring_send(0, right_order[p], True)
+        ring_send(0, left_order[p], False)
     send(head, hs.at[own], hx_send.at[0], hx_recv.at[0], at(1, 0))
     send(head, hs.at[own], hx_send.at[1], hx_recv.at[1], at(-1, 0))
     to_y(0, head)
     to_core(0, 0, head)
-    fs[z] = feat[...]
-    hs[own] = head[...]
-
-    behind = slot(-way, 0)
-    arrived(hs.at[behind], hx_recv.at[core])
-    send(hs.at[behind], hs.at[behind], hx_send.at[2], hx_recv.at[2], at(way, 0))
-    ahead = slot(way, 0)
-    arrived(hs.at[ahead], hx_recv.at[1 - core])
-    for j in (1, 2):
-        to_y(j, hs.at[slot(x_off[j], 0)])
-        to_core(j, 0, hs.at[slot(x_off[j], 0)])
-    ring_step(1)
-    arrived(hs.at[slot(2, 0)], hx_recv.at[2])
-    to_y(3, hs.at[slot(2, 0)])
-    to_core(3, 0, hs.at[slot(2, 0)])
+    mine = [
+        pltpu.make_async_copy(feat, fs.at[z], local.at[0]),
+        pltpu.make_async_copy(head, hs.at[own], local.at[1]),
+        pltpu.make_async_copy(cap_in, cap, local.at[2]),
+    ]
+    for c in mine:
+        c.start()
+
+    def x_near():
+        behind = slot(-way, 0)
+        arrived(hs.at[behind], hx_recv.at[core])
+        send(hs.at[behind], hs.at[behind], hx_send.at[2], hx_recv.at[2], at(way, 0))
+        arrived(hs.at[slot(way, 0)], hx_recv.at[1 - core])
+        for j in (1, 2):
+            to_y(j, hs.at[slot(x_off[j], 0)])
+            to_core(j, 0, hs.at[slot(x_off[j], 0)])
+
+    def x_far():
+        arrived(hs.at[slot(2, 0)], hx_recv.at[2])
+        to_y(3, hs.at[slot(2, 0)])
+        to_core(3, 0, hs.at[slot(2, 0)])
 
     def y_pair(j):
         k = slot(x_off[j], -way)
@@ -144,43 +157,51 @@
         arrived(hs.at[k], hy_recv.at[j, 2])
         to_core(j, 3, hs.at[k])
 
+    x_near()
+    ring_step(1)
     y_pair(0)
-    ring_step(2)
+    ring_step(2, range(PIECES // 2))
+    x_far()
+    ring_step(2, range(PIECES // 2, PIECES))
     y_far(0)
     y_pair(1)
-    ring_step(3)
+    ring_step(3, range(PIECES // 2))
+    y_pair(2)
+    ring_step(3, range(PIECES // 2, PIECES))
     y_far(1)
-    y_pair(2)
-    ring_step(4)
+    y_pair(3)
+    ring_step(4, range(PIECES // 2))
     y_far(2)
-    y_pair(3)
+    ring_step(4, range(PIECES // 2, PIECES))
+    y_far(3)
     ring_step(5)
-    y_far(3)
 
     def head_of(k):
         return hs[pl.ds(2 * k, 2)].reshape(slab, classes)
 
-    def logits_of(a, b, r0, n):
-        left = jnp.concatenate([fs[a, pl.ds(r0, n), :], fs[b, pl.ds(r0, n), :]], axis=1)
-        right = jnp.concatenate([head_of(a), head_of(b)], axis=0)
+    def logits_of(slots, r0, count):
+        left = jnp.concatenate([fs[k, pl.ds(r0, count), :] for k in slots], axis=1)
+        right = jnp.concatenate([head_of(k) for k in slots], axis=0)
         return jnp.dot(left, right, preferred_element_type=F32)
 
-    def around(d):
-        return lax.rem(z - d + groups, groups), lax.rem(z + d, groups)
-
-    ring_step(6)
+    def around(*distances):
+        return [lax.rem(z + d, groups) for e in distances for d in (groups - e, e)]
+
     for j in range(4):
         for i in range(4):
             k = (lax.rem(x + x_off[j] + SIDE, SIDE) * SIDE + lax.rem(y + x_off[i] + SIDE, SIDE)) * 2 + (1 - core)
             arrived(hs.at[k], hc_recv.at[j, i])
-    acc[...] = logits_of(*around(1), 0, rows)
-    for d in (2, 3, 4):
-        acc[...] += logits_of(*around(d), 0, rows)
-    ring_step(7)
-    for d in (5, 6, 7):
-        acc[...] += logits_of(*around(d), 0, rows)
-    ring_wait(far - 1, 0, True)
-    ring_wait(far - 1, 1, False)
+    for c in mine:
+        c.wait()
+    acc[...] = logits_of(around(1, 2), 0, rows)
+    ring_step(6, range(PIECES // 2))
+    acc[...] += logits_of(around(3, 4), 0, rows)
+    ring_step(6, range(PIECES // 2, PIECES))
+    acc[...] += logits_of(around(5), 0, rows)
+    ring_step(7, range(PIECES // 2))
+    acc[...] += logits_of(around(6), 0, rows)
+    ring_step(7, range(PIECES // 2, PIECES))
+    acc[...] += logits_of(around(7), 0, rows)
 
     lanes = 128
     tiles = classes // lanes
@@ -192,16 +213,19 @@
         return jnp.sum(sum(lane_tiles(v)[1:], lane_tiles(v)[0]).T, axis=0, keepdims=True)
 
     opposite = lax.rem(z + far, groups)
-    for r0 in range(0, rows, lanes):
-        block = pl.ds(r0, lanes)
-        tanh = jnp.tanh((acc[block, :] + logits_of(z, opposite, r0, lanes)) / softcap)
+    start_order = [q for pair in zip(right_order[: PIECES // 2], left_order[: PIECES // 2]) for q in pair]
+    for q in start_order:
+        ring_wait(far - 1, q, halfway(q, True))
+        r0 = q * n
+        block = pl.ds(r0, n)
+        tanh = jnp.tanh((acc[block, :] + logits_of([z, opposite], r0, n)) / softcap)
         student = jnp.exp(softcap * tanh)
         transport = student * student
         stu[block, :] = student
         plan[block, :] = transport
         slope[block, :] = 1.0 - tanh * tanh
-        zs0[:, r0:r0 + lanes] = turned_sum(transport)
-        zs0[:, rows + r0:rows + r0 + lanes] = turned_sum(student)
+        zs0[:, r0:r0 + n] = turned_sum(transport)
+        zs0[:, rows + r0:rows + r0 + n] = turned_sum(student)
 
     z_order = sorted(range(1, groups), key=lambda d: -min(d, groups - d))
 
@@ -235,7 +259,7 @@
 
     lax.fori_loop(0, groups, turn, 0)
 
-    ceiling = cap[...].astype(F32) * ratio
+    ceiling = cap[...].astype(F32).reshape(1, classes) * ratio
     scale = jnp.ones((1, classes), F32)
     both = z_total(zs0, zr0, 0)
     mass = both[:, :rows]
@@ -256,57 +280,62 @@
         z_exchange(zs.at[it], zr.at[it], it + 1)
         mass = z_total(zs.at[it], zr.at[it], it + 1)
 
+    def rs_send_to(d, q, right):
+        i = 0 if right else 1
+        src = part.at[d if right or d == far else groups - d]
+        dst = from_l if right else from_r
+        send(part_of(src, q), part_of(dst.at[d - 1], q), rs_send.at[i, d - 1, q], rs_recv.at[i, d - 1, q],
+             along(1 if right else -1))
+
+    def rs_add(d, q, right):
+        i = 0 if right else 1
+        got = (from_l if right else from_r).at[d]
+        mine = part.at[d if right else groups - d]
+        arrived(part_of(got, q), rs_recv.at[i, d, q])
+        block = pl.ds(q * n, n)
+        mine[block, :] = (mine[block, :].astype(F32) + got[block, :].astype(F32)).astype(BF)
+        rs_send_to(d, q, right)
+
+    def rs_step(d):
+        if d == far - 1:
+            pairs = [(right_order[p], left_order[p]) for p in range(PIECES // 2)]
+        else:
+            pairs = [(left_order[p], right_order[p]) for p in range(PIECES)]
+        for to_right, to_left in pairs:
+            rs_add(d, to_right, True)
+            rs_add(d, to_left, False)
+
+    def share_pair(d, r0=0, count=rows):
+        right = lax.rem(z + d, groups)
+        left = lax.rem(z - d + groups, groups) if d < far else z
+        both = jnp.concatenate([ht[right], ht[left]], axis=1)
+        block = pl.ds(r0, count)
+        out = jnp.dot(grad[block, :], both, preferred_element_type=F32).astype(BF)
+        part[d, block, :] = out[:, :slab]
+        part[groups - d if d < far else 0, block, :] = out[:, slab:]
+
     inverse = 1.0 / mass
     student_inverse = 1.0 / student_mass
-    for r0 in range(0, rows, lanes):
-        block = pl.ds(r0, lanes)
+    for q in start_order:
+        r0 = q * n
+        block = pl.ds(r0, n)
         up = jnp.concatenate([upright(inverse, r0)] * tiles, axis=1)
         sup = jnp.concatenate([upright(student_inverse, r0)] * tiles, axis=1)
         targets = (plan[block, :] * up * scale).astype(BF)
         tgt[block, :] = targets
         grad[block, :] = ((stu[block, :] * sup - targets.astype(F32)) * slope[block, :]).astype(BF)
-
-    def share_pair(d):
-        right = lax.rem(z + d, groups)
-        left = lax.rem(z - d + groups, groups) if d < far else z
-        both = jnp.concatenate([ht[right], ht[left]], axis=1)
-        out = jnp.dot(grad[...], both, preferred_element_type=F32).astype(BF)
-        part[d] = out[:, :slab]
-        part[groups - d if d < far else 0] = out[:, slab:]
-
-    def rs_send_to(d, h, right):
-        i = 0 if right else 1
-        src = part.at[d if right or d == far else groups - d]
-        dst = from_l if right else from_r
-        send(part_of(src, h), part_of(dst.at[d - 1], h), rs_send.at[i, d - 1, h], rs_recv.at[i, d - 1, h],
-             along(1 if right else -1))
-
-    def rs_add(d, h, right):
-        i = 0 if right else 1
-        got = (from_l if right else from_r).at[d]
-        mine = part.at[d if right else groups - d]
-        arrived(part_of(got, h), rs_recv.at[i, d, h])
-        at_h = pl.ds(h * half, half)
-        mine[at_h, :] = (mine[at_h, :].astype(F32) + got[at_h, :].astype(F32)).astype(BF)
-        rs_send_to(d, h, right)
-
-    def rs_step(d):
-        for h in range(2):
-            for right in (True, False):
-                if d < far - 1 or (h == 0) == right:
-                    rs_add(d, h, right)
+        share_pair(far, r0, n)
+        rs_send_to(far, q, halfway(q, True))
 
     def head_share(c, i):
         lhs = ft[c, lax.rem(y + i, SIDE)].reshape(SIDE * slab // 2, rows)
         out = jnp.dot(lhs, grad[...], preferred_element_type=F32).astype(BF)
         return out.reshape(SIDE, slab // 2, classes)
 
-    share_pair(far)
-    rs_send_to(far, 0, True)
-    rs_send_to(far, 1, False)
     share_pair(far - 1)
-    rs_send_to(far - 1, 1, True)
-    rs_send_to(far - 1, 0, False)
+    for p in range(PIECES // 2):
+        rs_send_to(far - 1, left_order[p], True)
+        rs_send_to(far - 1, right_order[p], False)
     for i in (2, 1, 3, 0):
         qo[i] = head_share(1 - core, i)
         send(qo.at[i], core_in.at[i], qc_send.at[i], qc_recv.at[i], at(0, 0, 1))
@@ -359,9 +388,9 @@
     arrived(x_in.at[1], qx_recv.at[1])
     arrived(x_in.at[2], qx_recv.at[2])
     ghead[...] = summed(qb[x], x_in[1], x_in[2])
-    for h in range(2):
-        arrived(part_of(from_l.at[0], h), rs_recv.at[0, 0, h])
-        arrived(part_of(from_r.at[0], h), rs_recv.at[1, 0, h])
+    for p in range(PIECES):
+        arrived(part_of(from_l.at[0], left_order[p]), rs_recv.at[0, 0, left_order[p]])
+        arrived(part_of(from_r.at[0], right_order[p]), rs_recv.at[1, 0, right_order[p]])
     gfeat[...] = summed(part[0], from_l[0], from_r[0])
 
     copy(zr0, zr0, zsend.at[0], zrecv.at[0], along(1)).wait_send()
@@ -370,6 +399,26 @@
         copy(cr.at[it], cr.at[it], csend.at[it], crecv.at[it], along(1)).wait_send()
     for c in sent:
         c.wait_send()
+
+
+def store_kernel(*refs):
+    count = len(refs) // 2
+    copies = [pltpu.make_async_copy(refs[i], refs[count + i], refs[-1].at[i]) for i in range(count)]
+    for c in copies:
+        c.start()
+    for c in copies:
+        c.wait()
+
+
+def store(results):
+    return pl.pallas_call(
+        store_kernel,
+        out_shape=tuple(jax.ShapeDtypeStruct(r.shape, r.dtype) for r in results),
+        in_specs=[pl.BlockSpec(memory_space=pltpu.VMEM)] * len(results),
+        out_specs=(pl.BlockSpec(memory_space=pltpu.HBM),) * len(results),
+        scratch_shapes=[pltpu.SemaphoreType.DMA((len(results),))],
+        compiler_params=pltpu.CompilerParams(vmem_limit_bytes=4 << 20),
+    )(*results)
 
 
 def solution(mesh):
@@ -389,7 +438,7 @@
             V((groups, rows, slab), BF), V((samples, depth, classes), BF),
             V((2, SIDE, SIDE, depth, rows), BF), V((groups, classes, slab), BF),
             V((rows, classes), F32), V((rows, classes), F32), V((rows, classes), F32), V((rows, classes), F32),
-            V((rows, classes), BF), V((8, 128), F32),
+            V((rows, classes), BF),
             V((groups, rows, slab), BF), V((far, rows, slab), BF), V((far, rows, slab), BF),
             V((SIDE, SIDE, depth, classes), BF), V((SIDE, SIDE, depth, classes), BF),
             V((SIDE, SIDE, depth, classes), BF), V((3, SIDE, depth, classes), BF),
@@ -397,25 +446,28 @@
             V((1, 2 * rows), F32), V((ITERS, 1, rows), F32),
             V((groups - 1, 1, 2 * rows), F32), V((ITERS, groups - 1, 1, rows), F32),
             V((ITERS, 1, classes), F32), V((ITERS, samples - 1, 1, classes), F32),
-            dma((2, far, 2)), dma((2, far, 2)), dma((3,)), dma((3,)), dma((4, 3)), dma((4, 3)), dma((4, 4)), dma((4, 4)),
+            dma((2, far, PIECES)), dma((2, far, PIECES)), dma((3,)), dma((3,)), dma((4, 3)), dma((4, 3)), dma((4, 4)), dma((4, 4)),
             dma((ITERS + 1,)), dma((ITERS + 1,)), dma((ITERS,)), dma((ITERS,)),
-            dma((2, far, 2)), dma((2, far, 2)), dma((4,)), dma((4,)), dma((3,)), dma((3,)), dma((3,)), dma((3,)),
+            V((classes,), BF), dma((3,)),
+            dma((2, far, PIECES)), dma((2, far, PIECES)), dma((4,)), dma((4,)), dma((3,)), dma((3,)), dma((3,)), dma((3,)),
         ]
         vmem = pl.BlockSpec(memory_space=pltpu.VMEM)
-        return pl.pallas_call(
+        hbm = pl.BlockSpec(memory_space=pltpu.HBM)
+        results = pl.pallas_call(
             functools.partial(kernel, rows, width, classes, groups, ratio),
             out_shape=(
                 jax.ShapeDtypeStruct((rows, classes), BF),
                 jax.ShapeDtypeStruct((rows, slab), BF),
                 jax.ShapeDtypeStruct((depth, classes), BF),
             ),
-            in_specs=[vmem] * 3,
+            in_specs=[hbm] * 3,
             out_specs=(vmem,) * 3,
             scratch_shapes=scratch,
             compiler_params=pltpu.CompilerParams(
                 collective_id=0, has_side_effects=True, vmem_limit_bytes=48 << 20
             ),
-        )(features, head, class_cap.reshape(1, classes))
+        )(features, head, class_cap)
+        return store(results)
 
     return jax.shard_map(
         per_device,

time: 127 us -> 122 us (0.961)
  the two profiles are of different devices: /device:TPU:8 before, /device:TPU:2 now
where the time goes in v2:
time: 122 us
  Pallas kernels  119 us (98%)
  local copies, waits for them, and re-layouts  2.41 us (2%)
    pallas_call x1, Pallas kernels, per_device(): pl.pallas_call(functools.partial(kernel, rows, width, classes, groups, ra...  118 us

profile of v2, /device:TPU:2, one launch (start us, length us, event | category | flops | bytes accessed | tf_op | source)
XLA Modules:
  0.0 121.6 jit_solution(1331091540783077876)
XLA Ops:
  0.6 0.0 copy-start
  0.6 0.9 copy-done
  1.5 0.0 copy-start.1
  1.5 0.8 copy-done.1
  2.4 0.0 copy-start.2
  2.4 0.7 copy-done.2
  3.1 117.7 %shard_map.58 = (bf16[512,512]{1,0:T(8,128)(2,1)S(1)}, bf16[512,128]{1,0:T(8,128)(2,1)S(1)}, bf16[64,512]{1,0:T(8,128)(2,1)S(1)}) custom-call(bf16[512,128]{1,0:T(8,128)(2,1)S(1)} %copy-done, bf16[64,512]{1,0:T(8,128)(2,1)S(1)} %copy-done.1, bf16[512]{0:T(512)(128)(2,1)S(1)} %copy-done.2), custom_call_target="tpu_custom_call" | custom-call | tf_op jit(solution)/shard_map/pallas_call | solution.py:456
  120.7 0.9 shard_map.59
Async XLA Ops:
  0.6 0.9 copy-start
  1.5 0.8 copy-start.1
  2.4 0.7 copy-start.2

commit v3 on v2

--- a/solution.py
+++ b/solution.py
@@ -25,13 +25,13 @@
     rows, width, classes, groups, ratio,
     feat, head, cap_in,
     tgt, gfeat, ghead,
-    fs, hs, ft, ht, acc, stu, plan, slope, grad,
+    fs, hs, fta, ftb, ht, acc, stu, plan, slope, grad,
     part, from_l, from_r,
-    qo, core_in, qa, y_in, qb, x_in,
+    qo, core_in, qa, first_in, qb, second_in,
     zs0, zs, zr0, zr, cs, cr,
     ag_send, ag_recv, hx_send, hx_recv, hy_send, hy_recv, hc_send, hc_recv,
     zsend, zrecv, csend, crecv, cap, local,
-    rs_send, rs_recv, qc_send, qc_recv, qy_send, qy_recv, qx_send, qx_recv,
+    rs_send, rs_recv, qc_send, qc_recv, q1_send, q1_recv, q2_send, q2_recv,
 ):
     s = lax.axis_index("sample")
     z = lax.axis_index("cls")
@@ -43,6 +43,7 @@
     n = rows // PIECES
     slab = width // groups
     far = groups // 2
+    quarter = slab // 4
 
     def at(dx, dy, flip=0):
         c = lax.rem(core + flip, 2)
@@ -187,6 +188,7 @@
     def around(*distances):
         return [lax.rem(z + d, groups) for e in distances for d in (groups - e, e)]
 
+    ring_step(6)
     for j in range(4):
         for i in range(4):
             k = (lax.rem(x + x_off[j] + SIDE, SIDE) * SIDE + lax.rem(y + x_off[i] + SIDE, SIDE)) * 2 + (1 - core)
@@ -194,12 +196,9 @@
     for c in mine:
         c.wait()
     acc[...] = logits_of(around(1, 2), 0, rows)
-    ring_step(6, range(PIECES // 2))
     acc[...] += logits_of(around(3, 4), 0, rows)
-    ring_step(6, range(PIECES // 2, PIECES))
-    acc[...] += logits_of(around(5), 0, rows)
     ring_step(7, range(PIECES // 2))
-    acc[...] += logits_of(around(6), 0, rows)
+    acc[...] += logits_of(around(5, 6), 0, rows)
     ring_step(7, range(PIECES // 2, PIECES))
     acc[...] += logits_of(around(7), 0, rows)
 
@@ -252,8 +251,9 @@
 
     def turn(k, carry):
         t = fs[k].T
-        ft[0, lax.rem(k, SIDE), k // SIDE] = t[: slab // 2]
-        ft[1, lax.rem(k, SIDE), k // SIDE] = t[slab // 2:]
+        for c in range(2):
+            fta[c, lax.rem(k, SIDE), k // SIDE] = t[(2 * c) * quarter:(2 * c + 1) * quarter]
+            ftb[c, k // SIDE, lax.rem(k, SIDE)] = t[(2 * c + 1) * quarter:(2 * c + 2) * quarter]
         ht[k] = head_of(k).T
         return carry
 
@@ -296,14 +296,8 @@
         mine[block, :] = (mine[block, :].astype(F32) + got[block, :].astype(F32)).astype(BF)
         rs_send_to(d, q, right)
 
-    def rs_step(d):
-        if d == far - 1:
-            pairs = [(right_order[p], left_order[p]) for p in range(PIECES // 2)]
-        else:
-            pairs = [(left_order[p], right_order[p]) for p in range(PIECES)]
-        for to_right, to_left in pairs:
-            rs_add(d, to_right, True)
-            rs_add(d, to_left, False)
+    rs_events = [(far - 1, right_order[p], left_order[p]) for p in range(PIECES // 2)]
+    rs_events += [(d, left_order[p], right_order[p]) for d in range(far - 2, 0, -1) for p in range(PIECES)]
 
     def share_pair(d, r0=0, count=rows):
         right = lax.rem(z + d, groups)
@@ -327,24 +321,10 @@
         share_pair(far, r0, n)
         rs_send_to(far, q, halfway(q, True))
 
-    def head_share(c, i):
-        lhs = ft[c, lax.rem(y + i, SIDE)].reshape(SIDE * slab // 2, rows)
-        out = jnp.dot(lhs, grad[...], preferred_element_type=F32).astype(BF)
-        return out.reshape(SIDE, slab // 2, classes)
-
     share_pair(far - 1)
     for p in range(PIECES // 2):
         rs_send_to(far - 1, left_order[p], True)
         rs_send_to(far - 1, right_order[p], False)
-    for i in (2, 1, 3, 0):
-        qo[i] = head_share(1 - core, i)
-        send(qo.at[i], core_in.at[i], qc_send.at[i], qc_recv.at[i], at(0, 0, 1))
-    share_pair(6)
-    rs_step(7)
-    for i in (2, 1, 3, 0):
-        qa[i] = head_share(core, i)
-    share_pair(5)
-    rs_step(6)
 
     def summed(*refs):
         out = refs[0].astype(F32)
@@ -354,40 +334,86 @@
 
     fwd = 1 + 2 * core
     bwd = 3 - 2 * core
-    for i in (2, 1, 3, 0):
-        arrived(core_in.at[i], qc_recv.at[i])
-        qa[i] = summed(qa[i], core_in[i])
-        if i == 2:
-            send(qa.at[2], y_in.at[0], qy_send.at[0], qy_recv.at[0], at(0, way))
-        if i == 3:
-            send(qa.at[bwd], y_in.at[1], qy_send.at[1], qy_recv.at[1], at(0, -way))
-    share_pair(4)
-    share_pair(3)
-    rs_step(5)
-    share_pair(2)
-    share_pair(1)
-    arrived(y_in.at[0], qy_recv.at[0])
-    qa[fwd] = summed(qa[fwd], y_in[0])
-    send(qa.at[fwd], y_in.at[2], qy_send.at[2], qy_recv.at[2], at(0, way))
-    rs_step(4)
-    rs_step(3)
-    arrived(y_in.at[1], qy_recv.at[1])
-    arrived(y_in.at[2], qy_recv.at[2])
-    qb[...] = summed(qa[0], y_in[1], y_in[2])
-
-    def x_of(d):
-        return lax.rem(x + d + SIDE, SIDE)
-
-    send(qb.at[x_of(2)], x_in.at[0], qx_send.at[0], qx_recv.at[0], at(way, 0))
-    send(qb.at[x_of(-way)], x_in.at[1], qx_send.at[1], qx_recv.at[1], at(-way, 0))
-    rs_step(2)
-    arrived(x_in.at[0], qx_recv.at[0])
-    qb[x_of(way)] = summed(qb[x_of(way)], x_in[0])
-    send(qb.at[x_of(way)], x_in.at[2], qx_send.at[2], qx_recv.at[2], at(way, 0))
-    rs_step(1)
-    arrived(x_in.at[1], qx_recv.at[1])
-    arrived(x_in.at[2], qx_recv.at[2])
-    ghead[...] = summed(qb[x], x_in[1], x_in[2])
+
+    def first_to(half, d):
+        return at(d, 0) if half else at(0, d)
+
+    def second_to(half, d):
+        return at(0, d) if half else at(d, 0)
+
+    def first_pos(half, d):
+        return lax.rem((x if half else y) + d + SIDE, SIDE)
+
+    def second_pos(half, d):
+        return lax.rem((y if half else x) + d + SIDE, SIDE)
+
+    def head_share(out, half, c, pair):
+        turned = ftb if half else fta
+        lhs = jnp.concatenate([turned[c, first_pos(half, i)].reshape(SIDE * quarter, rows) for i in pair], axis=0)
+        share = jnp.dot(lhs, grad[...], preferred_element_type=F32).astype(BF)
+        for n_, i in enumerate(pair):
+            out[half, i] = share[n_ * SIDE * quarter:(n_ + 1) * SIDE * quarter].reshape(SIDE, quarter, classes)
+
+    def give(half, pair):
+        head_share(qo, half, 1 - core, pair)
+        for i in pair:
+            send(qo.at[half, i], core_in.at[half, i], qc_send.at[half, i], qc_recv.at[half, i], at(0, 0, 1))
+
+    def keep(half):
+        head_share(qa, half, core, (2, 1))
+        head_share(qa, half, core, (3, 0))
+
+    def chip_sum(half):
+        for i in (2, 1, 3, 0):
+            arrived(core_in.at[half, i], qc_recv.at[half, i])
+            qa[half, i] = summed(qa[half, i], core_in[half, i])
+            if i == 2:
+                send(qa.at[half, 2], first_in.at[half, 0], q1_send.at[half, 0], q1_recv.at[half, 0], first_to(half, way))
+            if i == 3:
+                send(qa.at[half, bwd], first_in.at[half, 1], q1_send.at[half, 1], q1_recv.at[half, 1],
+                     first_to(half, -way))
+
+    def first_mid(half):
+        arrived(first_in.at[half, 0], q1_recv.at[half, 0])
+        qa[half, fwd] = summed(qa[half, fwd], first_in[half, 0])
+        send(qa.at[half, fwd], first_in.at[half, 2], q1_send.at[half, 2], q1_recv.at[half, 2], first_to(half, way))
+
+    def first_end(half):
+        arrived(first_in.at[half, 1], q1_recv.at[half, 1])
+        arrived(first_in.at[half, 2], q1_recv.at[half, 2])
+        qb[half] = summed(qa[half, 0], first_in[half, 1], first_in[half, 2])
+        send(qb.at[half, second_pos(half, 2)], second_in.at[half, 0], q2_send.at[half, 0], q2_recv.at[half, 0],
+             second_to(half, way))
+        send(qb.at[half, second_pos(half, -way)], second_in.at[half, 1], q2_send.at[half, 1], q2_recv.at[half, 1],
+             second_to(half, -way))
+
+    def second_mid(half):
+        arrived(second_in.at[half, 0], q2_recv.at[half, 0])
+        k = second_pos(half, way)
+        qb[half, k] = summed(qb[half, k], second_in[half, 0])
+        send(qb.at[half, k], second_in.at[half, 2], q2_send.at[half, 2], q2_recv.at[half, 2], second_to(half, way))
+
+    def second_end(half):
+        arrived(second_in.at[half, 1], q2_recv.at[half, 1])
+        arrived(second_in.at[half, 2], q2_recv.at[half, 2])
+        total = summed(qb[half, second_pos(half, 0)], second_in[half, 1], second_in[half, 2])
+        ghead[half * quarter:(half + 1) * quarter, :] = total
+
+    give(0, (2, 1))
+    give(0, (3, 0))
+    share_pair(6)
+    between = {
+        0: [(give, 1, (2, 1))], 1: [(give, 1, (3, 0))], 2: [(keep, 0)], 3: [(share_pair, 5)], 4: [(keep, 1), (chip_sum, 0)],
+        5: [(chip_sum, 1)], 6: [(share_pair, 4)], 7: [(share_pair, 3)], 8: [(share_pair, 2)], 9: [(share_pair, 1)],
+        11: [(first_mid, 0)], 12: [(first_mid, 1)], 16: [(first_end, 0)], 17: [(first_end, 1)],
+        20: [(second_mid, 0)], 21: [(second_mid, 1)], 25: [(second_end, 0), (second_end, 1)],
+    }
+    for e, (d, to_right, to_left) in enumerate(rs_events):
+        rs_add(d, to_right, True)
+        rs_add(d, to_left, False)
+        for task, *what in between.get(e, ()):
+            task(*what)
+
     for p in range(PIECES):
         arrived(part_of(from_l.at[0], left_order[p]), rs_recv.at[0, 0, left_order[p]])
         arrived(part_of(from_r.at[0], right_order[p]), rs_recv.at[1, 0, right_order[p]])
@@ -436,20 +462,20 @@
         dma = pltpu.SemaphoreType.DMA
         scratch = [
             V((groups, rows, slab), BF), V((samples, depth, classes), BF),
-            V((2, SIDE, SIDE, depth, rows), BF), V((groups, classes, slab), BF),
+            V((2, SIDE, SIDE, depth // 2, rows), BF), V((2, SIDE, SIDE, depth // 2, rows), BF), V((groups, classes, slab), BF),
             V((rows, classes), F32), V((rows, classes), F32), V((rows, classes), F32), V((rows, classes), F32),
             V((rows, classes), BF),
             V((groups, rows, slab), BF), V((far, rows, slab), BF), V((far, rows, slab), BF),
-            V((SIDE, SIDE, depth, classes), BF), V((SIDE, SIDE, depth, classes), BF),
-            V((SIDE, SIDE, depth, classes), BF), V((3, SIDE, depth, classes), BF),
-            V((SIDE, depth, classes), BF), V((3, depth, classes), BF),
+            V((2, SIDE, SIDE, depth // 2, classes), BF), V((2, SIDE, SIDE, depth // 2, classes), BF),
+            V((2, SIDE, SIDE, depth // 2, classes), BF), V((2, 3, SIDE, depth // 2, classes), BF),
+            V((2, SIDE, depth // 2, classes), BF), V((2, 3, depth // 2, classes), BF),
             V((1, 2 * rows), F32), V((ITERS, 1, rows), F32),
             V((groups - 1, 1, 2 * rows), F32), V((ITERS, groups - 1, 1, rows), F32),
             V((ITERS, 1, classes), F32), V((ITERS, samples - 1, 1, classes), F32),
             dma((2, far, PIECES)), dma((2, far, PIECES)), dma((3,)), dma((3,)), dma((4, 3)), dma((4, 3)), dma((4, 4)), dma((4, 4)),
             dma((ITERS + 1,)), dma((ITERS + 1,)), dma((ITERS,)), dma((ITERS,)),
             V((classes,), BF), dma((3,)),
-            dma((2, far, PIECES)), dma((2, far, PIECES)), dma((4,)), dma((4,)), dma((3,)), dma((3,)), dma((3,)), dma((3,)),
+            dma((2, far, PIECES)), dma((2, far, PIECES)), dma((2, 4)), dma((2, 4)), dma((2, 3)), dma((2, 3)), dma((2, 3)), dma((2, 3)),
         ]
         vmem = pl.BlockSpec(memory_space=pltpu.VMEM)
         hbm = pl.BlockSpec(memory_space=pltpu.HBM)
@@ -466,7 +492,7 @@
             compiler_params=pltpu.CompilerParams(
                 collective_id=0, has_side_effects=True, vmem_limit_bytes=48 << 20
             ),
-        )(features, head, class_cap)
+        )(*(pltpu.with_memory_space_constraint(a, pltpu.HBM) for a in (features, head, class_cap)))
         return store(results)
 
     return jax.shard_map(

time: 122 us -> 118 us (0.967)
  the two profiles are of different devices: /device:TPU:2 before, /device:TPU:32 now
where the time goes in v3:
time: 118 us
  Pallas kernels  117 us (99%)
    pallas_call x1, Pallas kernels, per_device(): pl.pallas_call(functools.partial(kernel, rows, width, classes, groups, ra...  116 us

profile of v3, /device:TPU:32, one launch (start us, length us, event | category | flops | bytes accessed | tf_op | source)
XLA Modules:
  0.0 118.0 jit_solution(18201469969518441677)
XLA Ops:
  0.6 116.4 %shard_map.58 = (bf16[512,512]{1,0:T(8,128)(2,1)S(1)}, bf16[512,128]{1,0:T(8,128)(2,1)S(1)}, bf16[64,512]{1,0:T(8,128)(2,1)S(1)}) custom-call(bf16[512,128]{1,0:T(8,128)(2,1)} %feat.1, bf16[64,512]{1,0:T(8,128)(2,1)} %head.1, bf16[512]{0:T(512)(128)(2,1)} %cap_in.1), custom_call_target="tpu_custom_call" | custom-call | tf_op jit(solution)/shard_map/pallas_call | solution.py:482
  117.1 0.9 shard_map.59

commit v4 on v3

--- a/solution.py
+++ b/solution.py
@@ -27,10 +27,11 @@
     tgt, gfeat, ghead,
     fs, hs, fta, ftb, ht, acc, stu, plan, slope, grad,
     part, from_l, from_r,
+    split, early, early_in, late,
     qo, core_in, qa, first_in, qb, second_in,
     zs0, zs, zr0, zr, cs, cr,
     ag_send, ag_recv, hx_send, hx_recv, hy_send, hy_recv, hc_send, hc_recv,
-    zsend, zrecv, csend, crecv, cap, local,
+    zsend, zrecv, csend, crecv, cap, local, e_send, e_recv,
     rs_send, rs_recv, qc_send, qc_recv, q1_send, q1_recv, q2_send, q2_recv,
 ):
     s = lax.axis_index("sample")
@@ -259,11 +260,79 @@
 
     lax.fori_loop(0, groups, turn, 0)
 
+    def early_share(w, r0, count):
+        block = pl.ds(r0, count)
+        early[w, 0, block, :] = jnp.dot(split[w, block, :], ht[opposite], preferred_element_type=F32).astype(BF)
+
+    def pair_share(w, d):
+        both = jnp.concatenate([ht[lax.rem(z + d, groups)], ht[lax.rem(z - d + groups, groups)]], axis=1)
+        return jnp.dot(split[w], both, preferred_element_type=F32)
+
+    def early_near(w):
+        out = pair_share(w, far - 1).astype(BF)
+        early[w, 1] = out[:, :slab]
+        early[w, 2] = out[:, slab:]
+
+    def early_send(w, level, q, right):
+        i = 0 if right else 1
+        src = early.at[w, 0 if level == 0 else 1 + i]
+        send(part_of(src, q), part_of(early_in.at[w, i, level], q), e_send.at[w, i, level, q],
+             e_recv.at[w, i, level, q], along(1 if right else -1))
+
+    def early_wait(w, level, q, right):
+        i = 0 if right else 1
+        arrived(part_of(early_in.at[w, i, level], q), e_recv.at[w, i, level, q])
+
+    def early_fresh(w):
+        for p in range(PIECES // 2):
+            early_send(w, 1, left_order[p], True)
+            early_send(w, 1, right_order[p], False)
+
+    def early_pass(w):
+        for p in range(PIECES // 2):
+            for q, right in ((right_order[p], True), (left_order[p], False)):
+                i = 0 if right else 1
+                early_wait(w, 0, q, right)
+                block = pl.ds(q * n, n)
+                added = early[w, 1 + i, block, :].astype(F32) + early_in[w, i, 0, block, :].astype(F32)
+                early[w, 1 + i, block, :] = added.astype(BF)
+                early_send(w, 1, q, right)
+
+    def late_shares(w):
+        for m, d in enumerate((far - 2, far - 3)):
+            late[w, m] = pair_share(w, d)
+
+    def while_columns_travel(it):
+        if it == 0:
+            for q in start_order:
+                block = pl.ds(q * n, n)
+                sup = jnp.concatenate([upright(student_inverse, q * n)] * tiles, axis=1)
+                split[0, block, :] = (stu[block, :] * sup * slope[block, :]).astype(BF)
+                early_share(0, q * n, n)
+                early_send(0, 0, q, halfway(q, True))
+            early_near(0)
+            early_fresh(0)
+        elif it == 1:
+            early_pass(0)
+        elif it == 2:
+            late_shares(0)
+
+    def while_last_rows_travel(scale):
+        for q in start_order:
+            block = pl.ds(q * n, n)
+            split[1, block, :] = (plan[block, :] * scale * slope[block, :]).astype(BF)
+            early_share(1, q * n, n)
+            early_send(1, 0, q, halfway(q, True))
+        early_near(1)
+        early_fresh(1)
+        late_shares(1)
+        early_pass(1)
+
     ceiling = cap[...].astype(F32).reshape(1, classes) * ratio
     scale = jnp.ones((1, classes), F32)
     both = z_total(zs0, zr0, 0)
     mass = both[:, :rows]
-    student_mass = both[:, rows:]
+    student_inverse = 1.0 / both[:, rows:]
     for it in range(ITERS):
         inverse = 1.0 / mass
         column = jnp.zeros((1, classes), F32)
@@ -273,11 +342,14 @@
             column += jnp.sum(plan[pl.ds(r0, lanes), :] * rep, axis=0, keepdims=True)
         cs[it] = column
         c_exchange(cs.at[it], cr.at[it], it)
+        while_columns_travel(it)
         total = c_total(cs.at[it], cr.at[it], it)
         scale = jnp.minimum(scale, ceiling / total)
         for r0 in range(0, rows, lanes):
             zs[it, :, r0:r0 + lanes] = turned_sum(plan[pl.ds(r0, lanes), :] * scale)
         z_exchange(zs.at[it], zr.at[it], it + 1)
+        if it == ITERS - 1:
+            while_last_rows_travel(scale)
         mass = z_total(zs.at[it], zr.at[it], it + 1)
 
     def rs_send_to(d, q, right):
@@ -296,35 +368,47 @@
         mine[block, :] = (mine[block, :].astype(F32) + got[block, :].astype(F32)).astype(BF)
         rs_send_to(d, q, right)
 
-    rs_events = [(far - 1, right_order[p], left_order[p]) for p in range(PIECES // 2)]
-    rs_events += [(d, left_order[p], right_order[p]) for d in range(far - 2, 0, -1) for p in range(PIECES)]
-
-    def share_pair(d, r0=0, count=rows):
-        right = lax.rem(z + d, groups)
-        left = lax.rem(z - d + groups, groups) if d < far else z
-        both = jnp.concatenate([ht[right], ht[left]], axis=1)
-        block = pl.ds(r0, count)
-        out = jnp.dot(grad[block, :], both, preferred_element_type=F32).astype(BF)
-        part[d, block, :] = out[:, :slab]
-        part[groups - d if d < far else 0, block, :] = out[:, slab:]
+    rs_events = [(d, left_order[p], right_order[p]) for d in range(far - 3, 0, -1) for p in range(PIECES)]
+
+    def share_pair(d):
+        both = jnp.concatenate([ht[lax.rem(z + d, groups)], ht[lax.rem(z - d + groups, groups)]], axis=1)
+        out = jnp.dot(grad[...], both, preferred_element_type=F32).astype(BF)
+        part[d] = out[:, :slab]
+        part[groups - d] = out[:, slab:]
+
+    def share_own():
+        part[0] = jnp.dot(grad[...], ht[z], preferred_element_type=F32).astype(BF)
 
     inverse = 1.0 / mass
-    student_inverse = 1.0 / student_mass
-    for q in start_order:
-        r0 = q * n
-        block = pl.ds(r0, n)
-        up = jnp.concatenate([upright(inverse, r0)] * tiles, axis=1)
-        sup = jnp.concatenate([upright(student_inverse, r0)] * tiles, axis=1)
+    ups = [upright(inverse, q * n) for q in range(PIECES)]
+
+    def merge(q, right):
+        i = 0 if right else 1
+        for w in range(2):
+            early_wait(w, 1, q, right)
+        block = pl.ds(q * n, n)
+        side = slice(i * slab, (i + 1) * slab)
+        student_part, plan_part = (late[w, 0, block, side] + early_in[w, i, 1, block, :].astype(F32) for w in range(2))
+        part[(far - 2) if right else groups - far + 2, block, :] = (student_part - ups[q] * plan_part).astype(BF)
+        rs_send_to(far - 2, q, right)
+
+    for p in range(PIECES // 2):
+        merge(left_order[p], True)
+        merge(right_order[p], False)
+    for q in range(PIECES):
+        block = pl.ds(q * n, n)
+        up = jnp.concatenate([ups[q]] * tiles, axis=1)
         targets = (plan[block, :] * up * scale).astype(BF)
         tgt[block, :] = targets
+        sup = jnp.concatenate([upright(student_inverse, q * n)] * tiles, axis=1)
         grad[block, :] = ((stu[block, :] * sup - targets.astype(F32)) * slope[block, :]).astype(BF)
-        share_pair(far, r0, n)
-        rs_send_to(far, q, halfway(q, True))
-
-    share_pair(far - 1)
-    for p in range(PIECES // 2):
-        rs_send_to(far - 1, left_order[p], True)
-        rs_send_to(far - 1, right_order[p], False)
+
+    def next_shares():
+        for q in range(PIECES):
+            block = pl.ds(q * n, n)
+            both = late[0, 1, block, :] - jnp.concatenate([ups[q]] * 2, axis=1) * late[1, 1, block, :]
+            part[far - 3, block, :] = both[:, :slab].astype(BF)
+            part[groups - far + 3, block, :] = both[:, slab:].astype(BF)
 
     def summed(*refs):
         out = refs[0].astype(F32)
@@ -401,12 +485,17 @@
 
     give(0, (2, 1))
     give(0, (3, 0))
-    share_pair(6)
+    give(1, (2, 1))
+    give(1, (3, 0))
+    for p in range(PIECES // 2, PIECES):
+        merge(left_order[p], True)
+        merge(right_order[p], False)
+    keep(0)
+    next_shares()
     between = {
-        0: [(give, 1, (2, 1))], 1: [(give, 1, (3, 0))], 2: [(keep, 0)], 3: [(share_pair, 5)], 4: [(keep, 1), (chip_sum, 0)],
-        5: [(chip_sum, 1)], 6: [(share_pair, 4)], 7: [(share_pair, 3)], 8: [(share_pair, 2)], 9: [(share_pair, 1)],
-        11: [(first_mid, 0)], 12: [(first_mid, 1)], 16: [(first_end, 0)], 17: [(first_end, 1)],
-        20: [(second_mid, 0)], 21: [(second_mid, 1)], 25: [(second_end, 0), (second_end, 1)],
+        0: [(keep, 1)], 1: [(chip_sum, 0)], 2: [(share_pair, 4), (chip_sum, 1)], 3: [(share_pair, 3)], 5: [(share_pair, 2)],
+        6: [(share_pair, 1)], 7: [(share_own,)], 8: [(first_mid, 0)], 9: [(first_mid, 1)],
+        13: [(first_end, 0)], 14: [(first_end, 1)], 17: [(second_mid, 0)], 18: [(second_mid, 1)],
     }
     for e, (d, to_right, to_left) in enumerate(rs_events):
         rs_add(d, to_right, True)
@@ -417,6 +506,8 @@
     for p in range(PIECES):
         arrived(part_of(from_l.at[0], left_order[p]), rs_recv.at[0, 0, left_order[p]])
         arrived(part_of(from_r.at[0], right_order[p]), rs_recv.at[1, 0, right_order[p]])
+    second_end(0)
+    second_end(1)
     gfeat[...] = summed(part[0], from_l[0], from_r[0])
 
     copy(zr0, zr0, zsend.at[0], zrecv.at[0], along(1)).wait_send()
@@ -466,6 +557,7 @@
             V((rows, classes), F32), V((rows, classes), F32), V((rows, classes), F32), V((rows, classes), F32),
             V((rows, classes), BF),
             V((groups, rows, slab), BF), V((far, rows, slab), BF), V((far, rows, slab), BF),
+            V((2, rows, classes), BF), V((2, 3, rows, slab), BF), V((2, 2, 2, rows, slab), BF), V((2, 2, rows, 2 * slab), F32),
             V((2, SIDE, SIDE, depth // 2, classes), BF), V((2, SIDE, SIDE, depth // 2, classes), BF),
             V((2, SIDE, SIDE, depth // 2, classes), BF), V((2, 3, SIDE, depth // 2, classes), BF),
             V((2, SIDE, depth // 2, classes), BF), V((2, 3, depth // 2, classes), BF),
@@ -474,7 +566,7 @@
             V((ITERS, 1, classes), F32), V((ITERS, samples - 1, 1, classes), F32),
             dma((2, far, PIECES)), dma((2, far, PIECES)), dma((3,)), dma((3,)), dma((4, 3)), dma((4, 3)), dma((4, 4)), dma((4, 4)),
             dma((ITERS + 1,)), dma((ITERS + 1,)), dma((ITERS,)), dma((ITERS,)),
-            V((classes,), BF), dma((3,)),
+            V((classes,), BF), dma((3,)), dma((2, 2, 2, PIECES)), dma((2, 2, 2, PIECES)),
             dma((2, far, PIECES)), dma((2, far, PIECES)), dma((2, 4)), dma((2, 4)), dma((2, 3)), dma((2, 3)), dma((2, 3)), dma((2, 3)),
         ]
         vmem = pl.BlockSpec(memory_space=pltpu.VMEM)

time: 118 us -> 114 us (0.966)
  the two profiles are of different devices: /device:TPU:32 before, /device:TPU:2 now
where the time goes in v4:
time: 114 us
  Pallas kernels  113 us (99%)
    pallas_call x1, Pallas kernels, per_device(): pl.pallas_call(functools.partial(kernel, rows, width, classes, groups, ra...  113 us

profile of v4, /device:TPU:2, one launch (start us, length us, event | category | flops | bytes accessed | tf_op | source)
XLA Modules:
  0.0 114.1 jit_solution(4017300025937137170)
XLA Ops:
  0.6 112.6 %shard_map.58 = (bf16[512,512]{1,0:T(8,128)(2,1)S(1)}, bf16[512,128]{1,0:T(8,128)(2,1)S(1)}, bf16[64,512]{1,0:T(8,128)(2,1)S(1)}) custom-call(bf16[512,128]{1,0:T(8,128)(2,1)} %feat.1, bf16[64,512]{1,0:T(8,128)(2,1)} %head.1, bf16[512]{0:T(512)(128)(2,1)} %cap_in.1), custom_call_target="tpu_custom_call" | custom-call | tf_op jit(solution)/shard_map/pallas_call | solution.py:574
  113.2 0.9 shard_map.59

commit v5 on v4

--- a/solution.py
+++ b/solution.py
@@ -25,9 +25,9 @@
     rows, width, classes, groups, ratio,
     feat, head, cap_in,
     tgt, gfeat, ghead,
-    fs, hs, fta, ftb, ht, acc, stu, plan, slope, grad,
+    fs, hs, fta, ftb, ht, acc, stu, plan, plan_t, slope, grad,
     part, from_l, from_r,
-    split, early, early_in, late,
+    split, early, early_in, late, beyond,
     qo, core_in, qa, first_in, qb, second_in,
     zs0, zs, zr0, zr, cs, cr,
     ag_send, ag_recv, hx_send, hx_recv, hy_send, hy_recv, hc_send, hc_recv,
@@ -67,6 +67,11 @@
         c = copy(src, dst, ssem, rsem, to)
         c.start()
         sent.append(c)
+
+    def flush(count):
+        for c in sent[:count]:
+            c.wait_send()
+        del sent[:count]
 
     def arrived(ref, rsem):
         copy(ref, ref, rsem, rsem, along(1)).wait_recv()
@@ -259,6 +264,10 @@
         return carry
 
     lax.fori_loop(0, groups, turn, 0)
+    for r0 in range(0, rows, lanes):
+        for c0 in range(0, classes, lanes):
+            plan_t[c0:c0 + lanes, r0:r0 + lanes] = plan[r0:r0 + lanes, c0:c0 + lanes].T
+    flush(len(sent))
 
     def early_share(w, r0, count):
         block = pl.ds(r0, count)
@@ -275,7 +284,7 @@
 
     def early_send(w, level, q, right):
         i = 0 if right else 1
-        src = early.at[w, 0 if level == 0 else 1 + i]
+        src = beyond.at[w, i] if level == 2 else early.at[w, 0 if level == 0 else 1 + i]
         send(part_of(src, q), part_of(early_in.at[w, i, level], q), e_send.at[w, i, level, q],
              e_recv.at[w, i, level, q], along(1 if right else -1))
 
@@ -301,6 +310,18 @@
     def late_shares(w):
         for m, d in enumerate((far - 2, far - 3)):
             late[w, m] = pair_share(w, d)
+
+    def side(right):
+        return slice(0, slab) if right else slice(slab, 2 * slab)
+
+    def early_further(w):
+        for p in range(PIECES // 2):
+            for q, right in ((left_order[p], True), (right_order[p], False)):
+                i = 0 if right else 1
+                early_wait(w, 1, q, right)
+                block = pl.ds(q * n, n)
+                beyond[w, i, block, :] = (late[w, 0, block, side(right)] + early_in[w, i, 1, block, :].astype(F32)).astype(BF)
+                early_send(w, 2, q, right)
 
     def while_columns_travel(it):
         if it == 0:
@@ -316,6 +337,7 @@
             early_pass(0)
         elif it == 2:
             late_shares(0)
+            early_further(0)
 
     def while_last_rows_travel(scale):
         for q in start_order:
@@ -327,6 +349,7 @@
         early_fresh(1)
         late_shares(1)
         early_pass(1)
+        early_further(1)
 
     ceiling = cap[...].astype(F32).reshape(1, classes) * ratio
     scale = jnp.ones((1, classes), F32)
@@ -335,12 +358,8 @@
     student_inverse = 1.0 / both[:, rows:]
     for it in range(ITERS):
         inverse = 1.0 / mass
-        column = jnp.zeros((1, classes), F32)
-        for r0 in range(0, rows, lanes):
-            up = upright(inverse, r0)
-            rep = jnp.concatenate([up] * tiles, axis=1)
-            column += jnp.sum(plan[pl.ds(r0, lanes), :] * rep, axis=0, keepdims=True)
-        cs[it] = column
+        for c0 in range(0, classes, lanes):
+            cs[it, :, c0:c0 + lanes] = turned_sum(plan_t[pl.ds(c0, lanes), :] * inverse)
         c_exchange(cs.at[it], cr.at[it], it)
         while_columns_travel(it)
         total = c_total(cs.at[it], cr.at[it], it)
@@ -368,7 +387,8 @@
         mine[block, :] = (mine[block, :].astype(F32) + got[block, :].astype(F32)).astype(BF)
         rs_send_to(d, q, right)
 
-    rs_events = [(d, left_order[p], right_order[p]) for d in range(far - 3, 0, -1) for p in range(PIECES)]
+    rs_events = [(far - 3, right_order[p], left_order[p]) for p in range(PIECES // 2)]
+    rs_events += [(d, left_order[p], right_order[p]) for d in range(far - 4, 0, -1) for p in range(PIECES)]
 
     def share_pair(d):
         both = jnp.concatenate([ht[lax.rem(z + d, groups)], ht[lax.rem(z - d + groups, groups)]], axis=1)
@@ -382,19 +402,18 @@
     inverse = 1.0 / mass
     ups = [upright(inverse, q * n) for q in range(PIECES)]
 
-    def merge(q, right):
+    def merge(q, right, level):
         i = 0 if right else 1
         for w in range(2):
-            early_wait(w, 1, q, right)
+            early_wait(w, level, q, right)
         block = pl.ds(q * n, n)
-        side = slice(i * slab, (i + 1) * slab)
-        student_part, plan_part = (late[w, 0, block, side] + early_in[w, i, 1, block, :].astype(F32) for w in range(2))
-        part[(far - 2) if right else groups - far + 2, block, :] = (student_part - ups[q] * plan_part).astype(BF)
-        rs_send_to(far - 2, q, right)
-
-    for p in range(PIECES // 2):
-        merge(left_order[p], True)
-        merge(right_order[p], False)
+        student_part, plan_part = (
+            late[w, level - 1, block, side(right)] + early_in[w, i, level, block, :].astype(F32) for w in range(2)
+        )
+        d = far - 1 - level
+        part[d if right else groups - d, block, :] = (student_part - ups[q] * plan_part).astype(BF)
+        rs_send_to(d, q, right)
+
     for q in range(PIECES):
         block = pl.ds(q * n, n)
         up = jnp.concatenate([ups[q]] * tiles, axis=1)
@@ -404,11 +423,10 @@
         grad[block, :] = ((stu[block, :] * sup - targets.astype(F32)) * slope[block, :]).astype(BF)
 
     def next_shares():
-        for q in range(PIECES):
-            block = pl.ds(q * n, n)
-            both = late[0, 1, block, :] - jnp.concatenate([ups[q]] * 2, axis=1) * late[1, 1, block, :]
-            part[far - 3, block, :] = both[:, :slab].astype(BF)
-            part[groups - far + 3, block, :] = both[:, slab:].astype(BF)
+        for p in range(PIECES // 2):
+            for q, right, k in ((right_order[p], True, far - 3), (left_order[p], False, groups - far + 3)):
+                block = pl.ds(q * n, n)
+                part[k, block, :] = (late[0, 1, block, side(right)] - ups[q] * late[1, 1, block, side(right)]).astype(BF)
 
     def summed(*refs):
         out = refs[0].astype(F32)
@@ -485,19 +503,29 @@
 
     give(0, (2, 1))
     give(0, (3, 0))
+    for p in range(PIECES // 2):
+        merge(right_order[p], True, 1)
+        merge(left_order[p], False, 1)
     give(1, (2, 1))
     give(1, (3, 0))
-    for p in range(PIECES // 2, PIECES):
-        merge(left_order[p], True)
-        merge(right_order[p], False)
     keep(0)
+    for p in range(PIECES // 2):
+        merge(left_order[p], True, 2)
+        merge(right_order[p], False, 2)
     next_shares()
+    keep(1)
+    chip_sum(0)
     between = {
-        0: [(keep, 1)], 1: [(chip_sum, 0)], 2: [(share_pair, 4), (chip_sum, 1)], 3: [(share_pair, 3)], 5: [(share_pair, 2)],
-        6: [(share_pair, 1)], 7: [(share_own,)], 8: [(first_mid, 0)], 9: [(first_mid, 1)],
-        13: [(first_end, 0)], 14: [(first_end, 1)], 17: [(second_mid, 0)], 18: [(second_mid, 1)],
+        0: [(share_pair, 4)], 1: [(chip_sum, 1)], 3: [(share_pair, 3)], 4: [(share_pair, 2)], 5: [(share_pair, 1)],
+        6: [(share_own,)], 7: [(first_mid, 0)], 8: [(first_mid, 1)], 12: [(first_end, 0)], 13: [(first_end, 1)],
+        16: [(second_mid, 0)], 17: [(second_mid, 1)],
     }
+    old = 0
     for e, (d, to_right, to_left) in enumerate(rs_events):
+        if e == 4:
+            old = len(sent)
+        if e == 12:
+            flush(old)
         rs_add(d, to_right, True)
         rs_add(d, to_left, False)
         for task, *what in between.get(e, ()):
@@ -514,13 +542,18 @@
     for it in range(ITERS):
         copy(zr.at[it], zr.at[it], zsend.at[it + 1], zrecv.at[it + 1], along(1)).wait_send()
         copy(cr.at[it], cr.at[it], csend.at[it], crecv.at[it], along(1)).wait_send()
-    for c in sent:
-        c.wait_send()
+    flush(len(sent))
 
 
 def store_kernel(*refs):
     count = len(refs) // 2
-    copies = [pltpu.make_async_copy(refs[i], refs[count + i], refs[-1].at[i]) for i in range(count)]
+    copies = []
+    for i in range(count):
+        parts = 4 if i == 0 else 1
+        rows = refs[i].shape[0] // parts
+        for p in range(parts):
+            block = pl.ds(p * rows, rows)
+            copies.append(pltpu.make_async_copy(refs[i].at[block], refs[count + i].at[block], refs[-1].at[len(copies)]))
     for c in copies:
         c.start()
     for c in copies:
@@ -533,7 +566,7 @@
         out_shape=tuple(jax.ShapeDtypeStruct(r.shape, r.dtype) for r in results),
         in_specs=[pl.BlockSpec(memory_space=pltpu.VMEM)] * len(results),
         out_specs=(pl.BlockSpec(memory_space=pltpu.HBM),) * len(results),
-        scratch_shapes=[pltpu.SemaphoreType.DMA((len(results),))],
+        scratch_shapes=[pltpu.SemaphoreType.DMA((len(results) + 3,))],
         compiler_params=pltpu.CompilerParams(vmem_limit_bytes=4 << 20),
     )(*results)
 
@@ -554,10 +587,12 @@
         scratch = [
             V((groups, rows, slab), BF), V((samples, depth, classes), BF),
             V((2, SIDE, SIDE, depth // 2, rows), BF), V((2, SIDE, SIDE, depth // 2, rows), BF), V((groups, classes, slab), BF),
-            V((rows, classes), F32), V((rows, classes), F32), V((rows, classes), F32), V((rows, classes), F32),
+            V((rows, classes), F32), V((rows, classes), F32), V((rows, classes), F32), V((classes, rows), F32),
+            V((rows, classes), F32),
             V((rows, classes), BF),
             V((groups, rows, slab), BF), V((far, rows, slab), BF), V((far, rows, slab), BF),
-            V((2, rows, classes), BF), V((2, 3, rows, slab), BF), V((2, 2, 2, rows, slab), BF), V((2, 2, rows, 2 * slab), F32),
+            V((2, rows, classes), BF), V((2, 3, rows, slab), BF), V((2, 2, 3, rows, slab), BF), V((2, 2, rows, 2 * slab), F32),
+            V((2, 2, rows, slab), BF),
             V((2, SIDE, SIDE, depth // 2, classes), BF), V((2, SIDE, SIDE, depth // 2, classes), BF),
             V((2, SIDE, SIDE, depth // 2, classes), BF), V((2, 3, SIDE, depth // 2, classes), BF),
             V((2, SIDE, depth // 2, classes), BF), V((2, 3, depth // 2, classes), BF),
@@ -566,7 +601,7 @@
             V((ITERS, 1, classes), F32), V((ITERS, samples - 1, 1, classes), F32),
             dma((2, far, PIECES)), dma((2, far, PIECES)), dma((3,)), dma((3,)), dma((4, 3)), dma((4, 3)), dma((4, 4)), dma((4, 4)),
             dma((ITERS + 1,)), dma((ITERS + 1,)), dma((ITERS,)), dma((ITERS,)),
-            V((classes,), BF), dma((3,)), dma((2, 2, 2, PIECES)), dma((2, 2, 2, PIECES)),
+            V((classes,), BF), dma((3,)), dma((2, 2, 3, PIECES)), dma((2, 2, 3, PIECES)),
             dma((2, far, PIECES)), dma((2, far, PIECES)), dma((2, 4)), dma((2, 4)), dma((2, 3)), dma((2, 3)), dma((2, 3)), dma((2, 3)),
         ]
         vmem = pl.BlockSpec(memory_space=pltpu.VMEM)

time: 114 us -> 114 us (level)
  no operation moved by 1% of the time
where the time goes in v5:
time: 114 us
  Pallas kernels  113 us (99%)
    pallas_call x1, Pallas kernels, per_device(): pl.pallas_call(functools.partial(kernel, rows, width, classes, groups, ra...  112 us

profile of v5, /device:TPU:2, one launch (start us, length us, event | category | flops | bytes accessed | tf_op | source)
XLA Modules:
  0.0 113.5 jit_solution(13815015587114746075)
XLA Ops:
  0.6 112.0 %shard_map.58 = (bf16[512,512]{1,0:T(8,128)(2,1)S(1)}, bf16[512,128]{1,0:T(8,128)(2,1)S(1)}, bf16[64,512]{1,0:T(8,128)(2,1)S(1)}) custom-call(bf16[512,128]{1,0:T(8,128)(2,1)} %feat.1, bf16[64,512]{1,0:T(8,128)(2,1)} %head.1, bf16[512]{0:T(512)(128)(2,1)} %cap_in.1), custom_call_target="tpu_custom_call" | custom-call | tf_op jit(solution)/shard_map/pallas_call | solution.py:609
  112.6 0.9 shard_map.59

commit v6 on v5

--- a/solution.py
+++ b/solution.py
@@ -30,7 +30,7 @@
     split, early, early_in, late, beyond,
     qo, core_in, qa, first_in, qb, second_in,
     zs0, zs, zr0, zr, cs, cr,
-    ag_send, ag_recv, hx_send, hx_recv, hy_send, hy_recv, hc_send, hc_recv,
+    ag_send, ag_recv, h_send, hx_recv, hy_recv, hc_recv,
     zsend, zrecv, csend, crecv, cap, local, e_send, e_recv,
     rs_send, rs_recv, qc_send, qc_recv, q1_send, q1_recv, q2_send, q2_recv,
 ):
@@ -61,17 +61,11 @@
             src_ref=src, dst_ref=dst, send_sem=ssem, recv_sem=rsem, device_id=to, device_id_type=MESH
         )
 
-    sent = []
-
     def send(src, dst, ssem, rsem, to):
-        c = copy(src, dst, ssem, rsem, to)
-        c.start()
-        sent.append(c)
-
-    def flush(count):
-        for c in sent[:count]:
-            c.wait_send()
-        del sent[:count]
+        copy(src, dst, ssem, rsem, to).start()
+
+    def left(ref, ssem):
+        copy(ref, ref, ssem, ssem, along(1)).wait_send()
 
     def arrived(ref, rsem):
         copy(ref, ref, rsem, rsem, along(1)).wait_recv()
@@ -96,7 +90,7 @@
         k = lax.rem(z - hop * t + groups, groups)
         src = part_of(feat, q) if t == 0 else part_of(fs.at[k], q)
         i = 0 if forward else 1
-        send(src, part_of(fs.at[k], q), ag_send.at[i, t, q], ag_recv.at[i, t, q], along(hop))
+        send(src, part_of(fs.at[k], q), ag_send.at[0], ag_recv.at[i, t, q], along(hop))
 
     def ring_wait(t, q, forward):
         hop = 1 if forward else -1
@@ -115,18 +109,18 @@
 
     def to_y(j, src):
         k = slot(x_off[j], 0)
-        send(src, hs.at[k], hy_send.at[j, 0], hy_recv.at[j, 0], at(0, 1))
-        send(src, hs.at[k], hy_send.at[j, 1], hy_recv.at[j, 1], at(0, -1))
+        send(src, hs.at[k], h_send.at[0], hy_recv.at[j, 0], at(0, 1))
+        send(src, hs.at[k], h_send.at[0], hy_recv.at[j, 1], at(0, -1))
 
     def to_core(j, i, src):
         k = slot(x_off[j], x_off[i])
-        send(src, hs.at[k], hc_send.at[j, i], hc_recv.at[j, i], at(0, 0, 1))
+        send(src, hs.at[k], h_send.at[0], hc_recv.at[0], at(0, 0, 1))
 
     for p in range(PIECES):
         ring_send(0, right_order[p], True)
         ring_send(0, left_order[p], False)
-    send(head, hs.at[own], hx_send.at[0], hx_recv.at[0], at(1, 0))
-    send(head, hs.at[own], hx_send.at[1], hx_recv.at[1], at(-1, 0))
+    send(head, hs.at[own], h_send.at[0], hx_recv.at[0], at(1, 0))
+    send(head, hs.at[own], h_send.at[0], hx_recv.at[1], at(-1, 0))
     to_y(0, head)
     to_core(0, 0, head)
     mine = [
@@ -140,7 +134,7 @@
     def x_near():
         behind = slot(-way, 0)
         arrived(hs.at[behind], hx_recv.at[core])
-        send(hs.at[behind], hs.at[behind], hx_send.at[2], hx_recv.at[2], at(way, 0))
+        send(hs.at[behind], hs.at[behind], h_send.at[0], hx_recv.at[2], at(way, 0))
         arrived(hs.at[slot(way, 0)], hx_recv.at[1 - core])
         for j in (1, 2):
             to_y(j, hs.at[slot(x_off[j], 0)])
@@ -154,7 +148,7 @@
     def y_pair(j):
         k = slot(x_off[j], -way)
         arrived(hs.at[k], hy_recv.at[j, core])
-        send(hs.at[k], hs.at[k], hy_send.at[j, 2], hy_recv.at[j, 2], at(0, way))
+        send(hs.at[k], hs.at[k], h_send.at[0], hy_recv.at[j, 2], at(0, way))
         arrived(hs.at[slot(x_off[j], way)], hy_recv.at[j, 1 - core])
         to_core(j, 1, hs.at[slot(x_off[j], -1)])
         to_core(j, 2, hs.at[slot(x_off[j], 1)])
@@ -195,10 +189,7 @@
         return [lax.rem(z + d, groups) for e in distances for d in (groups - e, e)]
 
     ring_step(6)
-    for j in range(4):
-        for i in range(4):
-            k = (lax.rem(x + x_off[j] + SIDE, SIDE) * SIDE + lax.rem(y + x_off[i] + SIDE, SIDE)) * 2 + (1 - core)
-            arrived(hs.at[k], hc_recv.at[j, i])
+    arrived(hs.at[pl.ds(0, 4 * SIDE)], hc_recv.at[0])
     for c in mine:
         c.wait()
     acc[...] = logits_of(around(1, 2), 0, rows)
@@ -267,7 +258,8 @@
     for r0 in range(0, rows, lanes):
         for c0 in range(0, classes, lanes):
             plan_t[c0:c0 + lanes, r0:r0 + lanes] = plan[r0:r0 + lanes, c0:c0 + lanes].T
-    flush(len(sent))
+    left(fs.at[pl.ds(0, groups - 1)], ag_send.at[0])
+    left(hs.at[pl.ds(0, hs.shape[0] - 1)], h_send.at[0])
 
     def early_share(w, r0, count):
         block = pl.ds(r0, count)
@@ -285,12 +277,12 @@
     def early_send(w, level, q, right):
         i = 0 if right else 1
         src = beyond.at[w, i] if level == 2 else early.at[w, 0 if level == 0 else 1 + i]
-        send(part_of(src, q), part_of(early_in.at[w, i, level], q), e_send.at[w, i, level, q],
-             e_recv.at[w, i, level, q], along(1 if right else -1))
+        send(part_of(src, q), part_of(early_in.at[w, i, level], q), e_send.at[w],
+             e_recv.at[w, i, level % 2, q], along(1 if right else -1))
 
     def early_wait(w, level, q, right):
         i = 0 if right else 1
-        arrived(part_of(early_in.at[w, i, level], q), e_recv.at[w, i, level, q])
+        arrived(part_of(early_in.at[w, i, level], q), e_recv.at[w, i, level % 2, q])
 
     def early_fresh(w):
         for p in range(PIECES // 2):
@@ -375,7 +367,7 @@
         i = 0 if right else 1
         src = part.at[d if right or d == far else groups - d]
         dst = from_l if right else from_r
-        send(part_of(src, q), part_of(dst.at[d - 1], q), rs_send.at[i, d - 1, q], rs_recv.at[i, d - 1, q],
+        send(part_of(src, q), part_of(dst.at[d - 1], q), rs_send.at[0], rs_recv.at[i, d - 1, q],
              along(1 if right else -1))
 
     def rs_add(d, q, right):
@@ -459,7 +451,7 @@
     def give(half, pair):
         head_share(qo, half, 1 - core, pair)
         for i in pair:
-            send(qo.at[half, i], core_in.at[half, i], qc_send.at[half, i], qc_recv.at[half, i], at(0, 0, 1))
+            send(qo.at[half, i], core_in.at[half, i], qc_send.at[0], qc_recv.at[half, i], at(0, 0, 1))
 
     def keep(half):
         head_share(qa, half, core, (2, 1))
@@ -470,30 +462,30 @@
             arrived(core_in.at[half, i], qc_recv.at[half, i])
             qa[half, i] = summed(qa[half, i], core_in[half, i])
             if i == 2:
-                send(qa.at[half, 2], first_in.at[half, 0], q1_send.at[half, 0], q1_recv.at[half, 0], first_to(half, way))
+                send(qa.at[half, 2], first_in.at[half, 0], q1_send.at[0], q1_recv.at[half, 0], first_to(half, way))
             if i == 3:
-                send(qa.at[half, bwd], first_in.at[half, 1], q1_send.at[half, 1], q1_recv.at[half, 1],
+                send(qa.at[half, bwd], first_in.at[half, 1], q1_send.at[0], q1_recv.at[half, 1],
                      first_to(half, -way))
 
     def first_mid(half):
         arrived(first_in.at[half, 0], q1_recv.at[half, 0])
         qa[half, fwd] = summed(qa[half, fwd], first_in[half, 0])
-        send(qa.at[half, fwd], first_in.at[half, 2], q1_send.at[half, 2], q1_recv.at[half, 2], first_to(half, way))
+        send(qa.at[half, fwd], first_in.at[half, 2], q1_send.at[0], q1_recv.at[half, 2], first_to(half, way))
 
     def first_end(half):
         arrived(first_in.at[half, 1], q1_recv.at[half, 1])
         arrived(first_in.at[half, 2], q1_recv.at[half, 2])
         qb[half] = summed(qa[half, 0], first_in[half, 1], first_in[half, 2])
-        send(qb.at[half, second_pos(half, 2)], second_in.at[half, 0], q2_send.at[half, 0], q2_recv.at[half, 0],
+        send(qb.at[half, second_pos(half, 2)], second_in.at[half, 0], q2_send.at[0], q2_recv.at[half, 0],
              second_to(half, way))
-        send(qb.at[half, second_pos(half, -way)], second_in.at[half, 1], q2_send.at[half, 1], q2_recv.at[half, 1],
+        send(qb.at[half, second_pos(half, -way)], second_in.at[half, 1], q2_send.at[0], q2_recv.at[half, 1],
              second_to(half, -way))
 
     def second_mid(half):
         arrived(second_in.at[half, 0], q2_recv.at[half, 0])
         k = second_pos(half, way)
         qb[half, k] = summed(qb[half, k], second_in[half, 0])
-        send(qb.at[half, k], second_in.at[half, 2], q2_send.at[half, 2], q2_recv.at[half, 2], second_to(half, way))
+        send(qb.at[half, k], second_in.at[half, 2], q2_send.at[0], q2_recv.at[half, 2], second_to(half, way))
 
     def second_end(half):
         arrived(second_in.at[half, 1], q2_recv.at[half, 1])
@@ -520,12 +512,11 @@
         6: [(share_own,)], 7: [(first_mid, 0)], 8: [(first_mid, 1)], 12: [(first_end, 0)], 13: [(first_end, 1)],
         16: [(second_mid, 0)], 17: [(second_mid, 1)],
     }
-    old = 0
     for e, (d, to_right, to_left) in enumerate(rs_events):
-        if e == 4:
-            old = len(sent)
         if e == 12:
-            flush(old)
+            for w in range(2):
+                left(part.at[pl.ds(0, 4)], e_send.at[w])
+            left(qo, qc_send.at[0])
         rs_add(d, to_right, True)
         rs_add(d, to_left, False)
         for task, *what in between.get(e, ()):
@@ -542,7 +533,9 @@
     for it in range(ITERS):
         copy(zr.at[it], zr.at[it], zsend.at[it + 1], zrecv.at[it + 1], along(1)).wait_send()
         copy(cr.at[it], cr.at[it], csend.at[it], crecv.at[it], along(1)).wait_send()
-    flush(len(sent))
+    left(part.at[pl.ds(0, far + 3)], rs_send.at[0])
+    left(first_in, q1_send.at[0])
+    left(second_in, q2_send.at[0])
 
 
 def store_kernel(*refs):
@@ -599,10 +592,10 @@
             V((1, 2 * rows), F32), V((ITERS, 1, rows), F32),
             V((groups - 1, 1, 2 * rows), F32), V((ITERS, groups - 1, 1, rows), F32),
             V((ITERS, 1, classes), F32), V((ITERS, samples - 1, 1, classes), F32),
-            dma((2, far, PIECES)), dma((2, far, PIECES)), dma((3,)), dma((3,)), dma((4, 3)), dma((4, 3)), dma((4, 4)), dma((4, 4)),
+            dma((1,)), dma((2, far, PIECES)), dma((1,)), dma((3,)), dma((4, 3)), dma((1,)),
             dma((ITERS + 1,)), dma((ITERS + 1,)), dma((ITERS,)), dma((ITERS,)),
-            V((classes,), BF), dma((3,)), dma((2, 2, 3, PIECES)), dma((2, 2, 3, PIECES)),
-            dma((2, far, PIECES)), dma((2, far, PIECES)), dma((2, 4)), dma((2, 4)), dma((2, 3)), dma((2, 3)), dma((2, 3)), dma((2, 3)),
+            V((classes,), BF), dma((3,)), dma((2,)), dma((2, 2, 2, PIECES)),
+            dma((1,)), dma((2, far - 2, PIECES)), dma((1,)), dma((2, 4)), dma((1,)), dma((2, 3)), dma((1,)), dma((2, 3)),
         ]
         vmem = pl.BlockSpec(memory_space=pltpu.VMEM)
         hbm = pl.BlockSpec(memory_space=pltpu.HBM)

time: 114 us -> 111 us (0.974)
  Pallas kernels: 113 us -> 110 us
    pallas_call x1, Pallas kernels: 112 us -> 110 us  [per_device(): pl.pallas_call(functools.partial(kernel, rows, width, classes, groups, ra...]
where the time goes in v6:
time: 111 us
  Pallas kernels  110 us (99%)
    pallas_call x1, Pallas kernels, per_device(): pl.pallas_call(functools.partial(kernel, rows, width, classes, groups, ra...  110 us

profile of v6, /device:TPU:2, one launch (start us, length us, event | category | flops | bytes accessed | tf_op | source)
XLA Modules:
  0.0 111.0 jit_solution(14645440585957320499)
XLA Ops:
  0.6 109.5 %shard_map.58 = (bf16[512,512]{1,0:T(8,128)(2,1)S(1)}, bf16[512,128]{1,0:T(8,128)(2,1)S(1)}, bf16[64,512]{1,0:T(8,128)(2,1)S(1)}) custom-call(bf16[512,128]{1,0:T(8,128)(2,1)} %feat.1, bf16[64,512]{1,0:T(8,128)(2,1)} %head.1, bf16[512]{0:T(512)(128)(2,1)} %cap_in.1), custom_call_target="tpu_custom_call" | custom-call | tf_op jit(solution)/shard_map/pallas_call | solution.py:602
  110.1 0.9 shard_map.59

commit v7 on v6

--- a/solution.py
+++ b/solution.py
@@ -30,9 +30,9 @@
     split, early, early_in, late, beyond,
     qo, core_in, qa, first_in, qb, second_in,
     zs0, zs, zr0, zr, cs, cr,
-    ag_send, ag_recv, h_send, hx_recv, hy_recv, hc_recv,
-    zsend, zrecv, csend, crecv, cap, local, e_send, e_recv,
-    rs_send, rs_recv, qc_send, qc_recv, q1_send, q1_recv, q2_send, q2_recv,
+    ag_send, ring_recv, h_send, hx_recv, hy_recv, hc_recv,
+    zsend, zrecv, csend, crecv, cap, local, e_send,
+    rs_send, qc_send, qc_recv, q1_send, q1_recv, q2_send, q2_recv,
 ):
     s = lax.axis_index("sample")
     z = lax.axis_index("cls")
@@ -90,12 +90,12 @@
         k = lax.rem(z - hop * t + groups, groups)
         src = part_of(feat, q) if t == 0 else part_of(fs.at[k], q)
         i = 0 if forward else 1
-        send(src, part_of(fs.at[k], q), ag_send.at[0], ag_recv.at[i, t, q], along(hop))
+        send(src, part_of(fs.at[k], q), ag_send.at[0], ring_recv.at[i, t, q], along(hop))
 
     def ring_wait(t, q, forward):
         hop = 1 if forward else -1
         k = lax.rem(z - hop * (t + 1) + groups, groups)
-        arrived(part_of(fs.at[k], q), ag_recv.at[0 if forward else 1, t, q])
+        arrived(part_of(fs.at[k], q), ring_recv.at[0 if forward else 1, t, q])
 
     def ring_step(t, pieces=range(PIECES)):
         for p in pieces:
@@ -278,11 +278,11 @@
         i = 0 if right else 1
         src = beyond.at[w, i] if level == 2 else early.at[w, 0 if level == 0 else 1 + i]
         send(part_of(src, q), part_of(early_in.at[w, i, level], q), e_send.at[w],
-             e_recv.at[w, i, level % 2, q], along(1 if right else -1))
+             ring_recv.at[i, far - 2 + 2 * w + level % 2, q], along(1 if right else -1))
 
     def early_wait(w, level, q, right):
         i = 0 if right else 1
-        arrived(part_of(early_in.at[w, i, level], q), e_recv.at[w, i, level % 2, q])
+        arrived(part_of(early_in.at[w, i, level], q), ring_recv.at[i, far - 2 + 2 * w + level % 2, q])
 
     def early_fresh(w):
         for p in range(PIECES // 2):
@@ -367,14 +367,14 @@
         i = 0 if right else 1
         src = part.at[d if right or d == far else groups - d]
         dst = from_l if right else from_r
-        send(part_of(src, q), part_of(dst.at[d - 1], q), rs_send.at[0], rs_recv.at[i, d - 1, q],
+        send(part_of(src, q), part_of(dst.at[d - 1], q), rs_send.at[0], ring_recv.at[i, d - 1, q],
              along(1 if right else -1))
 
     def rs_add(d, q, right):
         i = 0 if right else 1
         got = (from_l if right else from_r).at[d]
         mine = part.at[d if right else groups - d]
-        arrived(part_of(got, q), rs_recv.at[i, d, q])
+        arrived(part_of(got, q), ring_recv.at[i, d, q])
         block = pl.ds(q * n, n)
         mine[block, :] = (mine[block, :].astype(F32) + got[block, :].astype(F32)).astype(BF)
         rs_send_to(d, q, right)
@@ -523,8 +523,8 @@
             task(*what)
 
     for p in range(PIECES):
-        arrived(part_of(from_l.at[0], left_order[p]), rs_recv.at[0, 0, left_order[p]])
-        arrived(part_of(from_r.at[0], right_order[p]), rs_recv.at[1, 0, right_order[p]])
+        arrived(part_of(from_l.at[0], left_order[p]), ring_recv.at[0, 0, left_order[p]])
+        arrived(part_of(from_r.at[0], right_order[p]), ring_recv.at[1, 0, right_order[p]])
     second_end(0)
     second_end(1)
     gfeat[...] = summed(part[0], from_l[0], from_r[0])
@@ -592,10 +592,10 @@
             V((1, 2 * rows), F32), V((ITERS, 1, rows), F32),
             V((groups - 1, 1, 2 * rows), F32), V((ITERS, groups - 1, 1, rows), F32),
             V((ITERS, 1, classes), F32), V((ITERS, samples - 1, 1, classes), F32),
-            dma((1,)), dma((2, far, PIECES)), dma((1,)), dma((3,)), dma((4, 3)), dma((1,)),
+            dma((1,)), dma((2, far + 2, PIECES)), dma((1,)), dma((3,)), dma((4, 3)), dma((1,)),
             dma((ITERS + 1,)), dma((ITERS + 1,)), dma((ITERS,)), dma((ITERS,)),
-            V((classes,), BF), dma((3,)), dma((2,)), dma((2, 2, 2, PIECES)),
-            dma((1,)), dma((2, far - 2, PIECES)), dma((1,)), dma((2, 4)), dma((1,)), dma((2, 3)), dma((1,)), dma((2, 3)),
+            V((classes,), BF), dma((3,)), dma((2,)),
+            dma((1,)), dma((1,)), dma((2, 4)), dma((1,)), dma((2, 3)), dma((1,)), dma((2, 3)),
         ]
         vmem = pl.BlockSpec(memory_space=pltpu.VMEM)
         hbm = pl.BlockSpec(memory_space=pltpu.HBM)

time: 111 us -> 111 us (level)
  no operation moved by 1% of the time
where the time goes in v7:
time: 111 us; the launch traced here: 110 us
  Pallas kernels  110 us (99%)
    pallas_call x1, Pallas kernels, per_device(): pl.pallas_call(functools.partial(kernel, rows, width, classes, groups, ra...  109 us

profile of v7, /device:TPU:2, one launch (start us, length us, event | category | flops | bytes accessed | tf_op | source)
XLA Modules:
  0.0 110.5 jit_solution(14525886867807489232)
XLA Ops:
  0.6 108.9 %shard_map.58 = (bf16[512,512]{1,0:T(8,128)(2,1)S(1)}, bf16[512,128]{1,0:T(8,128)(2,1)S(1)}, bf16[64,512]{1,0:T(8,128)(2,1)S(1)}) custom-call(bf16[512,128]{1,0:T(8,128)(2,1)} %feat.1, bf16[64,512]{1,0:T(8,128)(2,1)} %head.1, bf16[512]{0:T(512)(128)(2,1)} %cap_in.1), custom_call_target="tpu_custom_call" | custom-call | tf_op jit(solution)/shard_map/pallas_call | solution.py:602
  109.6 0.9 shard_map.59
